TPU v7x, 32 devices: a whole 2x2x4 slice. The times are simulated.
32 devices in a mesh: dp: 8 (over z, x), mp: 4 (over y, core).
Axes of the slice: x: 2, y: 2, z: 4, core: 2. Of those that a mesh axis runs over, the one named last changes fastest.
Arguments:
- interface: float32 [8192, 512], P(('dp', 'mp')), may hold values from -6 to 6
- latents: float32 [1024, 1024], P(('dp', 'mp')), may hold values from -6 to 6
- keep_mask: int32 [8, 1024], P('dp'), may hold values from 0 to 1, as said below
- read_gain_lat: float32 [1024], replicated, may hold values from 0.25 to 1.75
- read_gain_int: float32 [512], replicated, may hold values from 0.25 to 1.75
- read_query: float32 [1024, 1024], P(None, 'mp'), may hold values from -0.1875 to 0.1875
- read_keyval: float32 [2, 512, 1024], P(None, None, 'mp'), may hold values from -0.25 to 0.25
- read_out: float32 [1024, 1024], P('mp'), may hold values from -3 to 3
- read_gain_mlp: float32 [1024], replicated, may hold values from 0.25 to 1.75
- read_up: float32 [1024, 4096], P(None, 'mp'), may hold values from -0.1875 to 0.1875
- read_down: float32 [4096, 1024], P('mp'), may hold values from -0.09375 to 0.09375
- self_gain_att: float32 [2, 1024], replicated, may hold values from 0.25 to 1.75
- self_qkv: float32 [2, 3, 1024, 1024], P(None, None, None, 'mp'), may hold values from -0.1875 to 0.1875
- self_out: float32 [2, 1024, 1024], P(None, 'mp'), may hold values from -1.5 to 1.5
- self_gain_mlp: float32 [2, 1024], replicated, may hold values from 0.25 to 1.75
- self_up: float32 [2, 1024, 4096], P(None, None, 'mp'), may hold values from -0.1875 to 0.1875
- self_down: float32 [2, 4096, 1024], P(None, 'mp'), may hold values from -0.09375 to 0.09375
- write_gain_int: float32 [512], replicated, may hold values from 0.25 to 1.75
- write_gain_lat: float32 [1024], replicated, may hold values from 0.25 to 1.75
- write_query: float32 [512, 512], P(None, 'mp'), may hold values from -0.25 to 0.25
- write_keyval: float32 [2, 1024, 512], P(None, None, 'mp'), may hold values from -0.1875 to 0.1875
- write_out: float32 [512, 512], P('mp'), may hold values from -1.5 to 1.5
- write_gain_mlp: float32 [512], replicated, may hold values from 0.25 to 1.75
- write_up: float32 [512, 2048], P(None, 'mp'), may hold values from -0.25 to 0.25
- write_down: float32 [2048, 512], P('mp'), may hold values from -0.125 to 0.125
- grad_interface_out: float32 [8192, 512], P(('dp', 'mp')), may hold values from -6 to 6
- grad_latents_out: float32 [1024, 1024], P(('dp', 'mp')), may hold values from -6 to 6
Outputs:
- interface_out: float32 [8192, 512], P(('dp', 'mp'))
- latents_out: float32 [1024, 1024], P(('dp', 'mp'))
- grad_interface: float32 [8192, 512], P(('dp', 'mp'))
- grad_latents: float32 [1024, 1024], P(('dp', 'mp'))
- grad_read_gain_lat: float32 [1024], replicated
- grad_read_gain_int: float32 [512], replicated
- grad_read_query: float32 [1024, 1024], P(None, 'mp')
- grad_read_keyval: float32 [2, 512, 1024], P(None, None, 'mp')
- grad_read_out: float32 [1024, 1024], P('mp')
- grad_read_gain_mlp: float32 [1024], replicated
- grad_read_up: float32 [1024, 4096], P(None, 'mp')
- grad_read_down: float32 [4096, 1024], P('mp')
- grad_self_gain_att: float32 [2, 1024], replicated
- grad_self_qkv: float32 [2, 3, 1024, 1024], P(None, None, None, 'mp')
- grad_self_out: float32 [2, 1024, 1024], P(None, 'mp')
- grad_self_gain_mlp: float32 [2, 1024], replicated
- grad_self_up: float32 [2, 1024, 4096], P(None, None, 'mp')
- grad_self_down: float32 [2, 4096, 1024], P(None, 'mp')
- grad_write_gain_int: float32 [512], replicated
- grad_write_gain_lat: float32 [1024], replicated
- grad_write_query: float32 [512, 512], P(None, 'mp')
- grad_write_keyval: float32 [2, 1024, 512], P(None, None, 'mp')
- grad_write_out: float32 [512, 512], P('mp')
- grad_write_gain_mlp: float32 [512], replicated
- grad_write_up: float32 [512, 2048], P(None, 'mp')
- grad_write_down: float32 [2048, 512], P('mp')
Inputs may be any that keep to these rules, and one draw needn't show every extreme that they name: `keep_mask`: each image keeps one patch or more.
All inputs are finite; a program needn't handle non-finite values.
Results may differ from a plain program's by a relative error of at most 0.0003.
Values sent between devices are 32-bit elements; how exact they have to be, the bound alone decides.
No kernel may reach another device: no remote copies, remote signals or barrier semaphores. Data moves between devices by JAX's collectives and lax.ppermute only.
A program may use at most 256 MiB of HBM per device.

v0:
```python
import math

import jax
import jax.numpy as jnp
from jax import lax
from jax.sharding import PartitionSpec as P

D = 1024
E = 512
HEADS = 16
LATENTS = 128
LAYERS = 2


EPSILON = 1e-05
PRECISE = lax.Precision.HIGHEST
MASK_FILL = -1000000000.0


def layer_norm(values, gain_vec):
    centre = jnp.mean(values, axis=-1, keepdims=True)
    centred = values - centre
    spread = jnp.mean(centred * centred, axis=-1, keepdims=True)
    return centred * lax.rsqrt(spread + EPSILON) * gain_vec


def product(left_side, right_side):
    return jnp.dot(left_side, right_side, precision=PRECISE)


def contract_rows(left_side, right_side):
    return lax.dot_general(left_side, right_side, (((0,), (0,)), ((), ())), precision=PRECISE)


def contract_last(left_side, right_side):
    return lax.dot_general(left_side, right_side, (((1,), (1,)), ((), ())), precision=PRECISE)


def attention(queries, keys_in, values_in, key_bias, images, head_width):
    query_len = queries.shape[0] // images
    key_len = keys_in.shape[0] // images
    head_count = queries.shape[1] // head_width
    query_heads = queries.reshape(images, query_len, head_count, head_width)
    key_heads = keys_in.reshape(images, key_len, head_count, head_width)
    value_heads = values_in.reshape(images, key_len, head_count, head_width)
    scores = jnp.einsum("bqhd,bkhd->bhqk", query_heads, key_heads, precision=PRECISE)
    scores = scores / math.sqrt(head_width) + key_bias[:, None, None, :]
    weights = jax.nn.softmax(scores, axis=-1)
    mixture = jnp.einsum("bhqk,bkhd->bqhd", weights, value_heads, precision=PRECISE)
    return mixture.reshape(images * query_len, head_count * head_width)


def attend_local(query_norm, key_norm, w_query, w_key, w_value, key_bias, head_width):
    return attention(
        product(query_norm, w_query),
        product(key_norm, w_key),
        product(key_norm, w_value),
        key_bias,
        key_bias.shape[0],
        head_width,
    )


def expand(norm_full, w_up):
    return jax.nn.gelu(product(norm_full, w_up))


def gather_rows(pieces_in):
    return lax.all_gather(pieces_in, "mp", axis=0, tiled=True)


def branch_sum(source, weight):
    return lax.psum_scatter(product(source, weight), "mp", scatter_dimension=0, tiled=True)


def spread_grad(grad_shard):
    return lax.all_gather(grad_shard, "mp", axis=0, tiled=True)


def collect_grads(pieces_in):
    return lax.psum_scatter(pieces_in, "mp", scatter_dimension=0, tiled=True)


def reduce_branch(weight_grads):
    return lax.psum(weight_grads, "dp")


def norm_backward(source, gain_vec, grad_normed):
    normed, pull_back = jax.vjp(layer_norm, source, gain_vec)
    return pull_back(grad_normed)


def norms_of(query_src, key_src, query_gain, key_gain, crossed):
    if crossed:
        gathered = gather_rows((layer_norm(query_src, query_gain), layer_norm(key_src, key_gain)))
        return (gathered[0], gathered[1])
    gathered = gather_rows((layer_norm(query_src, query_gain),))
    return (gathered[0], gathered[0])


def attend_forward(
    query_src,
    key_src,
    query_gain,
    key_gain,
    w_query,
    w_key,
    w_value,
    w_out,
    key_bias,
    head_width,
    crossed,
):
    query_norm, key_norm = norms_of(query_src, key_src, query_gain, key_gain, crossed)
    mixture = attend_local(query_norm, key_norm, w_query, w_key, w_value, key_bias, head_width)
    return (query_src + branch_sum(mixture, w_out), (query_norm, key_norm))


def attend_backward(
    grad_shard,
    query_src,
    key_src,
    query_gain,
    key_gain,
    w_query,
    w_key,
    w_value,
    w_out,
    key_bias,
    head_width,
    crossed,
):
    query_norm, key_norm = norms_of(query_src, key_src, query_gain, key_gain, crossed)
    if crossed:
        mixture, pull_back = jax.vjp(
            lambda query_in, key_in, query_weight, key_weight, value_weight: attend_local(
                query_in, key_in, query_weight, key_weight, value_weight, key_bias, head_width
            ),
            query_norm,
            key_norm,
            w_query,
            w_key,
            w_value,
        )
    else:
        mixture, pull_back = jax.vjp(
            lambda query_in, query_weight, key_weight, value_weight: attend_local(
                query_in, query_in, query_weight, key_weight, value_weight, key_bias, head_width
            ),
            query_norm,
            w_query,
            w_key,
            w_value,
        )
    grad_full = spread_grad(grad_shard)
    grad_out_weight = contract_rows(mixture, grad_full)
    pulled = pull_back(contract_last(grad_full, w_out))
    if crossed:
        query_part, key_part = collect_grads((pulled[0], pulled[1]))
        grad_query_src, gain_query = norm_backward(query_src, query_gain, query_part)
        grad_key_src, gain_key = norm_backward(key_src, key_gain, key_part)
        weight_grads = reduce_branch((pulled[2], pulled[3], pulled[4], grad_out_weight))
        return (grad_query_src, grad_key_src, (gain_query, gain_key), weight_grads)
    collected = collect_grads((pulled[0],))
    grad_query_src, gain_query = norm_backward(query_src, query_gain, collected[0])
    weight_grads = reduce_branch((pulled[1], pulled[2], pulled[3], grad_out_weight))
    return (grad_query_src, None, (gain_query,), weight_grads)


def expand_forward(stream, gain_vec, w_up, w_down):
    gathered = gather_rows((layer_norm(stream, gain_vec),))
    norm_full = gathered[0]
    return (stream + branch_sum(expand(norm_full, w_up), w_down), norm_full)


def expand_backward(grad_shard, stream, gain_vec, w_up, w_down):
    norm_full = gather_rows((layer_norm(stream, gain_vec),))[0]
    hidden, pull_back = jax.vjp(expand, norm_full, w_up)
    grad_full = spread_grad(grad_shard)
    grad_down = contract_rows(hidden, grad_full)
    grad_norm_full, grad_up = pull_back(contract_last(grad_full, w_down))
    collected = collect_grads((grad_norm_full,))
    grad_stream, grad_gain = norm_backward(stream, gain_vec, collected[0])
    return (grad_shard + grad_stream, grad_gain, reduce_branch((grad_up, grad_down)))


def body(
    interface,
    latents,
    keep_mask,
    read_gain_lat,
    read_gain_int,
    read_query,
    read_keyval,
    read_out,
    read_gain_mlp,
    read_up,
    read_down,
    self_gain_att,
    self_qkv,
    self_out,
    self_gain_mlp,
    self_up,
    self_down,
    write_gain_int,
    write_gain_lat,
    write_query,
    write_keyval,
    write_out,
    write_gain_mlp,
    write_up,
    write_down,
    grad_interface_out,
    grad_latents_out,
):
    images = keep_mask.shape[0]
    shard_rows = interface.shape[0]
    flat_keep = keep_mask.reshape(-1).astype(jnp.float32)
    keep_rows = lax.dynamic_slice_in_dim(
        flat_keep, lax.axis_index("mp") * shard_rows, shard_rows, 0
    )[:, None]
    stream_x0 = interface * keep_rows
    read_bias = jnp.where(keep_mask > 0, 0.0, MASK_FILL).astype(jnp.float32)
    open_bias = jnp.zeros((images, LATENTS), jnp.float32)
    latent_head = D // HEADS
    patch_head = E // HEADS
    stream_z1, read_stored = attend_forward(
        latents,
        stream_x0,
        read_gain_lat,
        read_gain_int,
        read_query,
        read_keyval[0],
        read_keyval[1],
        read_out,
        read_bias,
        latent_head,
        True,
    )
    stream_z, read_mlp_stored = expand_forward(stream_z1, read_gain_mlp, read_up, read_down)
    layer_store = []
    for layer_idx in range(LAYERS):
        attend_input = stream_z
        stream_mid, attend_stored = attend_forward(
            attend_input,
            attend_input,
            self_gain_att[layer_idx],
            self_gain_att[layer_idx],
            self_qkv[layer_idx, 0],
            self_qkv[layer_idx, 1],
            self_qkv[layer_idx, 2],
            self_out[layer_idx],
            open_bias,
            latent_head,
            False,
        )
        stream_z, expand_stored = expand_forward(
            stream_mid, self_gain_mlp[layer_idx], self_up[layer_idx], self_down[layer_idx]
        )
        layer_store.append((attend_input, attend_stored, stream_mid, expand_stored))
    stream_x1, write_stored = attend_forward(
        stream_x0,
        stream_z,
        write_gain_int,
        write_gain_lat,
        write_query,
        write_keyval[0],
        write_keyval[1],
        write_out,
        open_bias,
        patch_head,
        True,
    )
    interface_out, write_mlp_stored = expand_forward(
        stream_x1, write_gain_mlp, write_up, write_down
    )
    grad_x, gain_write_mlp, grads_write_mlp = expand_backward(
        grad_interface_out, stream_x1, write_gain_mlp, write_up, write_down
    )
    grad_query, grad_key, gains_write, grads_write = attend_backward(
        grad_x,
        stream_x0,
        stream_z,
        write_gain_int,
        write_gain_lat,
        write_query,
        write_keyval[0],
        write_keyval[1],
        write_out,
        open_bias,
        patch_head,
        True,
    )
    grad_x = grad_x + grad_query
    grad_z = grad_latents_out + grad_key
    gains_att_list = [None] * LAYERS
    gains_mlp_list = [None] * LAYERS
    grads_att_list = [None] * LAYERS
    grads_mlp_list = [None] * LAYERS
    for layer_idx in reversed(range(LAYERS)):
        attend_input, attend_stored, stream_mid, expand_stored = layer_store[layer_idx]
        grad_z, gain_mlp_layer, grads_mlp_layer = expand_backward(
            grad_z, stream_mid, self_gain_mlp[layer_idx], self_up[layer_idx], self_down[layer_idx]
        )
        grad_self, unused, gains_att_layer, grads_att_layer = attend_backward(
            grad_z,
            attend_input,
            attend_input,
            self_gain_att[layer_idx],
            self_gain_att[layer_idx],
            self_qkv[layer_idx, 0],
            self_qkv[layer_idx, 1],
            self_qkv[layer_idx, 2],
            self_out[layer_idx],
            open_bias,
            latent_head,
            False,
        )
        grad_z = grad_z + grad_self
        gains_att_list[layer_idx] = gains_att_layer[0]
        gains_mlp_list[layer_idx] = gain_mlp_layer
        grads_att_list[layer_idx] = grads_att_layer
        grads_mlp_list[layer_idx] = grads_mlp_layer
    grad_z, gain_read_mlp, grads_read_mlp = expand_backward(
        grad_z, stream_z1, read_gain_mlp, read_up, read_down
    )
    grad_query, grad_key, gains_read, grads_read = attend_backward(
        grad_z,
        latents,
        stream_x0,
        read_gain_lat,
        read_gain_int,
        read_query,
        read_keyval[0],
        read_keyval[1],
        read_out,
        read_bias,
        latent_head,
        True,
    )
    grad_z = grad_z + grad_query
    grad_x = grad_x + grad_key
    grad_interface = grad_x * keep_rows
    summed_gains = lax.psum(
        (
            gains_read[0],
            gains_read[1],
            gain_read_mlp,
            jnp.stack(gains_att_list),
            jnp.stack(gains_mlp_list),
            gains_write[0],
            gains_write[1],
            gain_write_mlp,
        ),
        ("dp", "mp"),
    )
    self_qkv_grad = jnp.stack(
        [jnp.stack([entry[0], entry[1], entry[2]]) for entry in grads_att_list]
    )
    self_out_grad = jnp.stack([entry[3] for entry in grads_att_list])
    self_up_grad = jnp.stack([entry[0] for entry in grads_mlp_list])
    self_down_grad = jnp.stack([entry[1] for entry in grads_mlp_list])
    weight_tuple = (
        grads_read[0],
        jnp.stack([grads_read[1], grads_read[2]]),
        grads_read[3],
        grads_read_mlp[0],
        grads_read_mlp[1],
        self_qkv_grad,
        self_out_grad,
        self_up_grad,
        self_down_grad,
        grads_write[0],
        jnp.stack([grads_write[1], grads_write[2]]),
        grads_write[3],
        grads_write_mlp[0],
        grads_write_mlp[1],
    )
    return (
        interface_out,
        stream_z,
        grad_interface,
        grad_z,
        summed_gains[0],
        summed_gains[1],
        weight_tuple[0],
        weight_tuple[1],
        weight_tuple[2],
        summed_gains[2],
        weight_tuple[3],
        weight_tuple[4],
        summed_gains[3],
        weight_tuple[5],
        weight_tuple[6],
        summed_gains[4],
        weight_tuple[7],
        weight_tuple[8],
        summed_gains[5],
        summed_gains[6],
        weight_tuple[9],
        weight_tuple[10],
        weight_tuple[11],
        summed_gains[7],
        weight_tuple[12],
        weight_tuple[13],
    )


def solution(mesh):
    in_specs = (
        P(("dp", "mp"), None),
        P(("dp", "mp"), None),
        P("dp", None),
        P(),
        P(),
        P(None, "mp"),
        P(None, None, "mp"),
        P("mp", None),
        P(),
        P(None, "mp"),
        P("mp", None),
        P(),
        P(None, None, None, "mp"),
        P(None, "mp", None),
        P(),
        P(None, None, "mp"),
        P(None, "mp", None),
        P(),
        P(),
        P(None, "mp"),
        P(None, None, "mp"),
        P("mp", None),
        P(),
        P(None, "mp"),
        P("mp", None),
        P(("dp", "mp"), None),
        P(("dp", "mp"), None),
    )
    out_specs = (
        P(("dp", "mp"), None),
        P(("dp", "mp"), None),
        P(("dp", "mp"), None),
        P(("dp", "mp"), None),
        P(),
        P(),
        P(None, "mp"),
        P(None, None, "mp"),
        P("mp", None),
        P(),
        P(None, "mp"),
        P("mp", None),
        P(),
        P(None, None, None, "mp"),
        P(None, "mp", None),
        P(),
        P(None, None, "mp"),
        P(None, "mp", None),
        P(),
        P(),
        P(None, "mp"),
        P(None, None, "mp"),
        P("mp", None),
        P(),
        P(None, "mp"),
        P("mp", None),
    )
    return jax.shard_map(body, mesh=mesh, in_specs=in_specs, out_specs=out_specs, check_vma=False)
```

profile of v0, /device:TPU:0, one launch (start us, length us, event | category | flops | bytes accessed | tf_op | source)
XLA Modules:
  0.0 2203.9 jit_solution(14452684715133826007)
XLA Ops:
  19.0 10.0 all_gather.65
  30.8 8.7 all-gather.6.cloned.1.call-done
  53.9 22.6 %reduce-scatter.19.cloned.1.call-done = f32[32,1024]{1,0:T(8,128)} async-done(((f32[128,1024]{1,0:T(8,128)}), f32[32,1024]{1,0:T(8,128)}) %reduce-scatter.19.cloned.1.call-update) | async-done | bytes 131088 | tf_op jit(solution)/shard_map/reduce_scatter | solution.py:73
  78.8 7.1 all_gather.66
  95.0 5.5 slice_bitcast_fusion
  108.2 8.9 reduce-scatter.21.cloned.1.call-done
  119.2 6.9 all_gather.67
  134.0 21.3 reduce-scatter.23.cloned.1.call-done
  157.2 7.0 all_gather.68
  169.8 5.5 fusion.10
  183.0 14.5 reduce-scatter.25.cloned.1.call-done
  199.6 6.9 all_gather.69
  214.3 21.4 reduce-scatter.27.cloned.1.call-done
  237.6 7.2 all_gather.70
  250.7 5.5 fusion.2
  267.3 18.1 reduce-scatter.29.cloned.1.call-done
  287.4 6.8 all_gather.71
  305.2 31.3 %reduce-scatter.31.cloned.1.call-done = f32[256,512]{1,0:T(8,128)} async-done(((f32[1024,512]{1,0:T(8,128)}), f32[256,512]{1,0:T(8,128)}) %reduce-scatter.31.cloned.1.call-update) | async-done | bytes 524304 | tf_op jit(solution)/shard_map/reduce_scatter | solution.py:73
  340.5 20.1 all-gather.12.cloned.1.call-done
  360.6 6.6 fusion.207
  367.2 18.2 all-gather.10.cloned.1.call-done
  385.5 9.6 fusion.29
  402.4 6.9 fusion.54
  409.4 23.4 %reduce-scatter.35.cloned.1.call-done = f32[256,512]{1,0:T(8,128)} async-done(((f32[1024,512]{1,0:T(8,128)}), f32[256,512]{1,0:T(8,128)}) %reduce-scatter.35.cloned.1.call-update) | async-done | bytes 524304 | tf_op jit(solution)/shard_map/reduce_scatter | solution.py:81
  435.9 31.4 %reduce-scatter.33.cloned.1.call-done = f32[256,512]{1,0:T(8,128)} async-done(((f32[1024,512]{1,0:T(8,128)}), f32[256,512]{1,0:T(8,128)}) %reduce-scatter.33.cloned.1.call-update) | async-done | bytes 524304 | tf_op jit(solution)/shard_map/reduce_scatter | solution.py:73
  470.5 22.7 %all-gather.14.cloned.1.call-done = f32[1024,512]{1,0:T(8,128)} async-done(((f32[256,512]{1,0:T(8,128)}), f32[1024,512]{1,0:T(8,128)}) %all-gather.14.cloned.1.call-update) | async-done | bytes 2097168 | tf_op jit(solution)/shard_map/all_gather | solution.py:77
  508.6 21.8 reduce-scatter.39.cloned.1.call-done
  533.9 7.2 all_gather.76
  541.0 6.9 fusion.75
  548.7 7.3 fusion.4
  559.4 18.9 reduce-scatter.41.cloned.1.call-done
  581.2 7.1 all_gather.77
  600.2 22.1 %reduce-scatter.43.cloned.1.call-done = f32[32,1024]{1,0:T(8,128)} async-done(((f32[128,1024]{1,0:T(8,128)}), f32[32,1024]{1,0:T(8,128)}) %reduce-scatter.43.cloned.1.call-update) | async-done | bytes 131088 | tf_op jit(solution)/shard_map/reduce_scatter | solution.py:81
  625.9 7.0 all_gather.78
  632.9 6.9 fusion.69
  640.6 7.4 fusion.12
  648.1 22.1 %reduce-scatter.45.cloned.1.call-done = f32[32,1024]{1,0:T(8,128)} async-done(((f32[128,1024]{1,0:T(8,128)}), f32[32,1024]{1,0:T(8,128)}) %reduce-scatter.45.cloned.1.call-update) | async-done | bytes 131088 | tf_op jit(solution)/shard_map/reduce_scatter | solution.py:81
  673.2 7.2 all_gather.79
  692.2 22.2 %reduce-scatter.47.cloned.1.call-done = f32[32,1024]{1,0:T(8,128)} async-done(((f32[128,1024]{1,0:T(8,128)}), f32[32,1024]{1,0:T(8,128)}) %reduce-scatter.47.cloned.1.call-update) | async-done | bytes 131088 | tf_op jit(solution)/shard_map/reduce_scatter | solution.py:81
  717.2 7.2 all_gather.80
  724.4 6.8 fusion.213
  738.1 21.5 reduce-scatter.49.cloned.1.call-done
  763.3 7.0 all_gather.81
  789.2 6.9 fusion.222
  868.4 5.5 fusion.178
  893.9 47.7 %all-reduce = (f32[1024]{0:T(1024)}, f32[512]{0:T(512)}, f32[1024]{0:T(1024)}, f32[2,1024]{1,0:T(2,128)}, f32[2,1024]{1,0:T(2,128)}, /*index=5*/f32[512]{0:T(512)}, f32[1024]{0:T(1024)}, f32[512]{0:T(512)}) all-reduce(f32[1024]{0:T(1024)S(1)} %get-tuple-element.48, ...), channel_id=1, replica_groups=mesh['dp'=8,'mp'=4] {'dp','mp'}, use_global_device_ids=true, to_apply=%region_69.70 | all-reduce | flops 8704 | bytes 69632 | tf_op jit(solution)/shard_map/psum | solution.py:344
  942.8 1218.9 %all-reduce.4.cloned.1.call-done = (f32[1024,256]{1,0:T(8,128)}, f32[1,512,256]{2,1,0:T(8,128)}, f32[1,512,256]{2,1,0:T(8,128)}, f32[256,1024]{1,0:T(8,128)}, f3...) async-done(((f32[1024,256]{1,0:T(8,128)}, ...) | async-done | bytes 40370192 | tf_op jit(solution)/shard_map/psum | solution.py:85
  2177.7 6.8 pad_maximum_fusion
  (814 shorter events, 339.5 us)
Async XLA Ops:
  7.2 378.3 %copy-start = (f32[512,512]{1,0:T(8,128)S(1)}, f32[512,512]{1,0:T(8,128)}, u32[]{:S(2)}) copy-start(f32[512,512]{1,0:T(8,128)} %param.50) | copy-start | bytes 3145732
  7.2 32.3 %all-gather.6.cloned.1.call-start = ((), (), s32[]{:S(2)}) async-start(), calls=%async_computation.18 | async-start | bytes 2621440 | tf_op jit(solution)/shard_map/all_gather | solution.py:69
  12.9 63.6 %reduce-scatter.19.cloned.1.call-start = ((), (), s32[]{:S(2)}) async-start(), calls=%async_computation.19 | async-start | bytes 655360 | tf_op jit(solution)/shard_map/reduce_scatter | solution.py:73
  53.8 63.3 %reduce-scatter.21.cloned.1.call-start = ((), (), s32[]{:S(2)}) async-start(), calls=%async_computation.20 | async-start | bytes 655360 | tf_op jit(solution)/shard_map/reduce_scatter | solution.py:73
  95.0 60.3 %reduce-scatter.23.cloned.1.call-start = ((), (), s32[]{:S(2)}) async-start(), calls=%async_computation.21 | async-start | bytes 655360 | tf_op jit(solution)/shard_map/reduce_scatter | solution.py:73
  108.2 91.2 %copy-start.183 = (f32[1,1024]{1,0:T(1,128)}, f32[1,1024]{1,0:T(1,128)S(1)}, u32[]{:S(2)}) copy-start(f32[1,1024]{1,0:T(1,128)S(1)} %get-tuple-element.131) | copy-start | bytes 12292
  133.2 64.3 %reduce-scatter.25.cloned.1.call-start = ((), (), s32[]{:S(2)}) async-start(), calls=%async_computation.22 | async-start | bytes 655360 | tf_op jit(solution)/shard_map/reduce_scatter | solution.py:73
  134.0 35.0 %copy-start.185 = (f32[1,1024]{1,0:T(1,128)}, f32[1,1024]{1,0:T(1,128)S(1)}, u32[]{:S(2)}) copy-start(f32[1,1024]{1,0:T(1,128)S(1)} %get-tuple-element.130) | copy-start | bytes 12292
  134.0 103.5 %copy-start.187 = (f32[1,1024]{1,0:T(1,128)}, f32[1,1024]{1,0:T(1,128)S(1)}, u32[]{:S(2)}) copy-start(f32[1,1024]{1,0:T(1,128)S(1)} %get-tuple-element.129) | copy-start | bytes 12292
  175.3 60.3 %reduce-scatter.27.cloned.1.call-start = ((), (), s32[]{:S(2)}) async-start(), calls=%async_computation.23 | async-start | bytes 655360 | tf_op jit(solution)/shard_map/reduce_scatter | solution.py:73
  213.5 49.2 %all-gather.8.cloned.1.call-start = ((), (), s32[]{:S(2)}) async-start(), calls=%async_computation.25 | async-start | bytes 2621440 | tf_op jit(solution)/shard_map/all_gather | solution.py:69
  214.2 71.2 %reduce-scatter.29.cloned.1.call-start = ((), (), s32[]{:S(2)}) async-start(), calls=%async_computation.24 | async-start | bytes 655360 | tf_op jit(solution)/shard_map/reduce_scatter | solution.py:73
  256.3 80.2 %reduce-scatter.31.cloned.1.call-start = ((), (), s32[]{:S(2)}) async-start(), calls=%async_computation.26 | async-start | bytes 2621440 | tf_op jit(solution)/shard_map/reduce_scatter | solution.py:73
  304.6 56.0 %all-gather.12.cloned.1.call-start = ((), (), s32[]{:S(2)}) async-start(), calls=%async_computation.29 | async-start | bytes 2621440 | tf_op jit(solution)/shard_map/all_gather | solution.py:77
  305.2 80.3 %all-gather.10.cloned.1.call-start = ((), (), s32[]{:S(2)}) async-start(), calls=%async_computation.27 | async-start | bytes 2621440 | tf_op jit(solution)/shard_map/all_gather | solution.py:69
  340.3 92.5 %reduce-scatter.35.cloned.1.call-start = ((), (), s32[]{:S(2)}) async-start(), calls=%async_computation.30 | async-start | bytes 2621440 | tf_op jit(solution)/shard_map/reduce_scatter | solution.py:81
  401.2 66.1 %reduce-scatter.33.cloned.1.call-start = ((), (), s32[]{:S(2)}) async-start(), calls=%async_computation.28 | async-start | bytes 2621440 | tf_op jit(solution)/shard_map/reduce_scatter | solution.py:73
  409.3 60.2 %copy-start.111 = (f32[256,512]{1,0:T(8,128)S(1)}, f32[256,512]{1,0:T(8,128)}, u32[]{:S(2)}) copy-start(f32[256,512]{1,0:T(8,128)} %param.52) | copy-start | bytes 1572868
  409.3 83.9 %all-gather.14.cloned.1.call-start = ((), (), s32[]{:S(2)}) async-start(), calls=%async_computation.31 | async-start | bytes 2621440 | tf_op jit(solution)/shard_map/all_gather | solution.py:77
  470.5 59.9 %reduce-scatter.39.cloned.1.call-start = ((), (), s32[]{:S(2)}) async-start(), calls=%async_computation.33 | async-start | bytes 655360 | tf_op jit(solution)/shard_map/reduce_scatter | solution.py:81
  507.0 34.0 %copy-start.34 = (f32[128,1024]{1,0:T(8,128)S(1)}, f32[128,1024]{1,0:T(8,128)}, u32[]{:S(2)}) copy-start(f32[128,1024]{1,0:T(8,128)} %copy-done.33) | copy-start | bytes 1572868
  508.5 69.7 %reduce-scatter.41.cloned.1.call-start = ((), (), s32[]{:S(2)}) async-start(), calls=%async_computation.34 | async-start | bytes 655360 | tf_op jit(solution)/shard_map/reduce_scatter | solution.py:81
  556.1 66.2 %reduce-scatter.43.cloned.1.call-start = ((), (), s32[]{:S(2)}) async-start(), calls=%async_computation.35 | async-start | bytes 655360 | tf_op jit(solution)/shard_map/reduce_scatter | solution.py:81
  559.3 30.0 %copy-start.107 = (f32[4,128,128]{1,2,0:T(8,128)S(1)}, f32[4,128,128]{1,2,0:T(8,128)}, u32[]{:S(2)}) copy-start(f32[4,128,128]{1,2,0:T(8,128)} %copy-done.106) | copy-start | bytes 786436
  559.3 30.0 %copy-start.207 = (f32[4,128]{1,0:T(4,128)S(1)}, f32[4,128]{1,0:T(4,128)}, u32[]{:S(2)}) copy-start(f32[4,128]{1,0:T(4,128)} %copy-done.206) | copy-start | bytes 6148
  594.3 29.7 %copy-start.265 = (f32[32]{0:T(128)S(1)}, f32[32]{0:T(128)}, u32[]{:S(2)}) copy-start(f32[32]{0:T(128)} %copy-done.264) | copy-start | bytes 388
  596.8 36.0 %copy-start.31 = (f32[128,1024]{1,0:T(8,128)S(1)}, f32[128,1024]{1,0:T(8,128)}, u32[]{:S(2)}) copy-start(f32[128,1024]{1,0:T(8,128)} %copy-done.30) | copy-start | bytes 1572868
  600.2 70.0 %reduce-scatter.45.cloned.1.call-start = ((), (), s32[]{:S(2)}) async-start(), calls=%async_computation.36 | async-start | bytes 655360 | tf_op jit(solution)/shard_map/reduce_scatter | solution.py:81
  640.5 29.7 %copy-start.54 = (f32[32,1024]{1,0:T(8,128)S(1)}, f32[32,1024]{1,0:T(8,128)}, u32[]{:S(2)}) copy-start(f32[32,1024]{1,0:T(8,128)} %copy-done.53) | copy-start | bytes 393220
  640.5 29.7 %copy-start.186 = (f32[1,1024]{1,0:T(1,128)S(1)}, f32[1,1024]{1,0:T(1,128)}, u32[]{:S(2)}) copy-start(f32[1,1024]{1,0:T(1,128)} %copy-done.185) | copy-start | bytes 12292
  640.5 29.7 %copy-start.230 = (f32[32]{0:T(128)S(1)}, f32[32]{0:T(128)}, u32[]{:S(2)}) copy-start(f32[32]{0:T(128)} %copy-done.229) | copy-start | bytes 388
  640.5 29.7 %copy-start.250 = (f32[32]{0:T(128)S(1)}, f32[32]{0:T(128)}, u32[]{:S(2)}) copy-start(f32[32]{0:T(128)} %copy-done.249) | copy-start | bytes 388
  640.5 31.4 %copy-start.263 = (f32[32]{0:T(128)S(1)}, f32[32]{0:T(128)}, u32[]{:S(2)}) copy-start(f32[32]{0:T(128)} %copy-done.262) | copy-start | bytes 388
  640.5 32.5 %copy-start.118 = (f32[32,1024]{1,0:T(8,128)S(1)}, f32[32,1024]{1,0:T(8,128)}, u32[]{:S(2)}) copy-start(f32[32,1024]{1,0:T(8,128)} %copy-done.117) | copy-start | bytes 393220
  648.0 33.4 %copy-start.105 = (f32[4,128,128]{1,2,0:T(8,128)S(1)}, f32[4,128,128]{1,2,0:T(8,128)}, u32[]{:S(2)}) copy-start(f32[4,128,128]{1,2,0:T(8,128)} %copy-done.104) | copy-start | bytes 786436
  648.0 33.4 %copy-start.205 = (f32[4,128]{1,0:T(4,128)S(1)}, f32[4,128]{1,0:T(4,128)}, u32[]{:S(2)}) copy-start(f32[4,128]{1,0:T(4,128)} %copy-done.204) | copy-start | bytes 6148
  648.0 66.4 %reduce-scatter.47.cloned.1.call-start = ((), (), s32[]{:S(2)}) async-start(), calls=%async_computation.37 | async-start | bytes 655360 | tf_op jit(solution)/shard_map/reduce_scatter | solution.py:81
  686.3 29.7 %copy-start.261 = (f32[32]{0:T(128)S(1)}, f32[32]{0:T(128)}, u32[]{:S(2)}) copy-start(f32[32]{0:T(128)} %copy-done.260) | copy-start | bytes 388
  692.1 67.5 %reduce-scatter.49.cloned.1.call-start = ((), (), s32[]{:S(2)}) async-start(), calls=%async_computation.38 | async-start | bytes 655360 | tf_op jit(solution)/shard_map/reduce_scatter | solution.py:81
  737.4 35.2 %copy-start.180 = (f32[1,1024]{1,0:T(1,128)S(1)}, f32[1,1024]{1,0:T(1,128)}, u32[]{:S(2)}) copy-start(f32[1,1024]{1,0:T(1,128)} %copy-done.179) | copy-start | bytes 12292
  737.4 35.3 %copy-start.200 = (f32[4,128]{1,0:T(4,128)S(1)}, f32[4,128]{1,0:T(4,128)}, u32[]{:S(2)}) copy-start(f32[4,128]{1,0:T(4,128)} %copy-done.199) | copy-start | bytes 6148
  737.5 149.8 %reduce-scatter.53.cloned.1.call-start = ((), (), s32[]{:S(2)}) async-start(), calls=%async_computation.40 | async-start | bytes 655360 | tf_op jit(solution)/shard_map/reduce_scatter | solution.py:81
  781.8 108.6 %reduce-scatter.37.cloned.1.call-start = ((), (), s32[]{:S(2)}) async-start(), calls=%async_computation.32 | async-start | bytes 2621440 | tf_op jit(solution)/shard_map/reduce_scatter | solution.py:81
  788.9 101.4 %reduce-scatter.51.cloned.1.call-start = ((), (), s32[]{:S(2)}) async-start(), calls=%async_computation.39 | async-start | bytes 2621440 | tf_op jit(solution)/shard_map/reduce_scatter | solution.py:81
  815.9 1345.8 %all-reduce.4.cloned.1.call-start = ((), (), s32[]{:S(2)}) async-start(), calls=%async_computation.41 | async-start | bytes 80740352 | tf_op jit(solution)/shard_map/psum | solution.py:85
  887.2 54.4 %copy-start.71 = (f32[256,512]{1,0:T(8,128)S(1)}, f32[256,512]{1,0:T(8,128)}, u32[]{:S(2)}) copy-start(f32[256,512]{1,0:T(8,128)} %add_add_fusion.3) | copy-start | bytes 1572868
  890.3 51.3 %copy-start.59 = (f32[256,512]{1,0:T(8,128)S(1)}, f32[256,512]{1,0:T(8,128)}, u32[]{:S(2)}) copy-start(f32[256,512]{1,0:T(8,128)} %reduce-scatter.37.cloned.1.call-done) | copy-start | bytes 1572868
  890.4 51.2 %copy-start.60 = (f32[256,512]{1,0:T(8,128)S(1)}, f32[256,512]{1,0:T(8,128)}, u32[]{:S(2)}) copy-start(f32[256,512]{1,0:T(8,128)} %reduce-scatter.51.cloned.1.call-done) | copy-start | bytes 1572868
  (247 other events, 1711.8 us)
Sparse Core Ops, SparseCore 0:
  13.0 26.4 all-gather.5
  54.0 22.4 reduce-scatter.18
  95.1 22.0 reduce-scatter.20
  133.3 21.9 reduce-scatter.22
  175.4 22.0 reduce-scatter.24
  213.6 22.0 reduce-scatter.26
  237.9 22.5 all-gather.7
  263.7 21.6 reduce-scatter.28
  304.7 31.7 reduce-scatter.30
  338.0 22.5 all-gather.11
  362.8 22.5 all-gather.9
  401.3 31.4 reduce-scatter.34
  435.9 31.3 reduce-scatter.32
  470.6 22.5 all-gather.13
  508.6 21.6 reduce-scatter.38
  556.2 22.0 reduce-scatter.40
  600.3 22.0 reduce-scatter.42
  648.1 22.0 reduce-scatter.44
  692.3 22.0 reduce-scatter.46
  737.6 22.0 reduce-scatter.48
  781.9 22.0 reduce-scatter.52
  806.5 31.4 reduce-scatter.36
  841.2 31.3 reduce-scatter.50
  886.7 1274.9 all-reduce.3
where the time goes:
time: 2220 us; the launch traced here: 2200 us
  waiting for transfers between devices  1610 us (73%)
  matrix products  284 us (13%)
  blocking collectives  142 us (6%)
  local copies, waits for them, and re-layouts  76.6 us (3%)
  other arithmetic  69.8 us (3%)
    psum x1, waiting for transfers between devices, reduce_branch(): return lax.psum(weight_grads, 'dp')  1220 us
    dot_general x56, matrix products, product(): return jnp.dot(left_side, right_side, precision=PRECISE)  186 us
    reduce_scatter x8, waiting for transfers between devices, branch_sum(): lax.psum_scatter(product(source, weight), 'mp', scatter_dimension=0, tile...  169 us
    reduce_scatter x10, waiting for transfers between devices, collect_grads(): return lax.psum_scatter(pieces_in, 'mp', scatter_dimension=0, tiled=True)  152 us
    all_gather x7, blocking collectives, gather_rows(): return lax.all_gather(pieces_in, 'mp', axis=0, tiled=True)  51.9 us
    psum x1, blocking collectives, body(): lax.psum((gains_read[0], gains_read[1], gain_read_mlp, jnp.stack(gains_at...  47.7 us
  transfers between devices with their start and end apart: 24, of which 20 were waited for; matrix products, arithmetic and copies ran while one was open for 8% of the time, Pallas kernels for 0%

commit v1 on v0

v1 whole, which is shorter than its diff:
```python
import functools
import math

import jax
import jax.numpy as jnp
from jax import lax
from jax.experimental import pallas as pl
from jax.experimental.pallas import tpu as pltpu
from jax.sharding import PartitionSpec as P

EPSILON = 1e-05
BF16 = jnp.bfloat16
F32 = jnp.float32
NN = (((1,), (0,)), ((), ()))
NT = (((1,), (1,)), ((), ()))
TN = (((0,), (0,)), ((), ()))
GELU_C = math.sqrt(2.0 / math.pi)
HEAD = 64
VMEM_BYTES = 58 * 1024 * 1024


def cut(value):
    high = value.astype(BF16)
    return high, (value - high.astype(F32)).astype(BF16)


def mul3(left, right, dims):
    one = functools.partial(lax.dot_general, dimension_numbers=dims, preferred_element_type=F32)
    return one(left[0], right[0]) + (one(left[1], right[0]) + one(left[0], right[1]))


def normed(value):
    centre = jnp.mean(value, axis=-1, keepdims=True)
    centred = value - centre
    scale = lax.rsqrt(jnp.mean(centred * centred, axis=-1, keepdims=True) + EPSILON)
    return centred * scale, scale


def norm_back(dy, value, gain):
    n, scale = normed(value)
    dn = dy * gain
    dv = (
        dn
        - jnp.mean(dn, axis=-1, keepdims=True)
        - n * jnp.mean(dn * n, axis=-1, keepdims=True)
    ) * scale
    return dv, jnp.sum(dy * n, axis=0, keepdims=True)


def gelu_parts(pre):
    square = pre * pre
    bend = jnp.tanh(GELU_C * pre * (1.0 + 0.044715 * square))
    half = 0.5 * (1.0 + bend)
    slope = half + 0.5 * pre * (1.0 - bend * bend) * (GELU_C * (1.0 + 3.0 * 0.044715 * square))
    return pre * half, slope


def head_masks(width, head):
    lane = lax.broadcasted_iota(jnp.int32, (1, width), 1)
    return [(lane // head == h).astype(F32) for h in range(width // head)]


def stack_heads(value, masks):
    return jnp.concatenate([value * mask for mask in masks], axis=0)


def merge_heads(stacked, masks):
    rows = stacked.shape[0] // len(masks)
    total = stacked[:rows] * masks[0]
    for h in range(1, len(masks)):
        total = total + stacked[h * rows : (h + 1) * rows] * masks[h]
    return total


def soft(scores):
    top = jnp.max(scores, axis=-1, keepdims=True)
    raised = jnp.exp(scores - top)
    return raised / jnp.sum(raised, axis=-1, keepdims=True)


def attend(q, k, v, masks, head, bias=None):
    qs = stack_heads(q, masks)
    scores = mul3(cut(qs), cut(k), NT) * (1.0 / math.sqrt(head))
    if bias is not None:
        scores = scores + bias
    p = soft(scores)
    return merge_heads(mul3(cut(p), cut(v), NN), masks), p, qs


def attend_back(q, k, v, do, masks, head):
    scale = 1.0 / math.sqrt(head)
    k2, v2 = cut(k), cut(v)
    qs = cut(stack_heads(q, masks))
    p = soft(mul3(qs, k2, NT) * scale)
    p2 = cut(p)
    mix = merge_heads(mul3(p2, v2, NN), masks)
    dos = cut(stack_heads(do, masks))
    dp = mul3(dos, v2, NT)
    ds = cut(p * (dp - jnp.sum(dp * p, axis=-1, keepdims=True)) * scale)
    dq = merge_heads(mul3(ds, k2, NN), masks)
    dk = mul3(ds, qs, TN)
    dv = mul3(p2, dos, TN)
    return mix, dq, dk, dv


def place_copies(where, sets, hi, lo, half, stage, sem):
    z_at, x_at, c_at = where[0], where[1], where[2]
    copies = []
    for flip_c in range(2):
        for flip_x in range(lo):
            ref = sets[flip_c * lo + flip_x]
            for d in range(hi):
                image = lax.rem(z_at + d, hi) * lo + lax.rem(x_at + flip_x, lo)
                row = (image * 2 + lax.rem(c_at + flip_c, 2)) * half
                row = pl.multiple_of(row, half)
                copies.append(
                    pltpu.make_async_copy(ref.at[d], stage.at[pl.ds(row, half)], sem)
                )
    return copies


def load_rows(where, z_sets, d_sets, gain, hi, lo, half, stage_z, stage_d, a, at, d2, sems):
    zc = place_copies(where, z_sets, hi, lo, half, stage_z, sems.at[0])
    dc = place_copies(where, d_sets, hi, lo, half, stage_d, sems.at[1])
    for one in zc:
        one.start()
    for one in dc:
        one.start()
    for one in zc:
        one.wait()
    rows = stage_z.shape[0]
    step = 128

    def norm_step(i, carry):
        at_rows = pl.ds(pl.multiple_of(i * step, step), step)
        n = normed(stage_z[at_rows, :])[0] * gain[...]
        a[0, at_rows, :], a[1, at_rows, :] = cut(n)
        at[0, :, at_rows], at[1, :, at_rows] = cut(n.T)
        return carry

    lax.fori_loop(0, rows // step, norm_step, 0)
    for one in dc:
        one.wait()

    def cut_step(i, carry):
        at_rows = pl.ds(pl.multiple_of(i * step, step), step)
        d2[0, at_rows, :], d2[1, at_rows, :] = cut(stage_d[at_rows, :])
        return carry

    lax.fori_loop(0, rows // step, cut_step, 0)


def mlp_weights_kernel(hi, lo, half, *refs):
    where = refs[0]
    z_sets, d_sets = refs[1:5], refs[5:9]
    gain, w_up, w_down = refs[9:12]
    g_up, g_down, stage_z, stage_d, a, at, d2, h2t, du2, sems = refs[-10:]
    rows = stage_z.shape[0]
    tile = w_up.shape[1]
    step = 256

    @pl.when(pl.program_id(0) == 0)
    def _():
        load_rows(where, z_sets, d_sets, gain, hi, lo, half, stage_z, stage_d, a, at, d2, sems)

    wu = cut(w_up[...])
    wd = cut(w_down[...])

    def rows_step(i, carry):
        r = pl.ds(pl.multiple_of(i * step, step), step)
        pre = mul3((a[0, r, :], a[1, r, :]), wu, NN)
        hidden, slope = gelu_parts(pre)
        du = mul3((d2[0, r, :], d2[1, r, :]), wd, NT) * slope
        du2[0, r, :], du2[1, r, :] = cut(du)
        h2t[0, :, r], h2t[1, :, r] = cut(hidden.T)
        return carry

    lax.fori_loop(0, rows // step, rows_step, 0)
    du = (du2[0], du2[1])
    width = g_up.shape[0]

    def up_step(i, carry):
        r = pl.ds(pl.multiple_of(i * step, step), step)
        g_up[r, :] = mul3((at[0, r, :], at[1, r, :]), du, NN)
        return carry

    lax.fori_loop(0, width // step, up_step, 0)
    ht = (h2t[0], h2t[1])

    def down_step(i, carry):
        r = pl.ds(pl.multiple_of(i * step, step), step)
        g_down[:, r] = mul3(ht, (d2[0, :, r], d2[1, :, r]), NN)
        return carry

    lax.fori_loop(0, width // step, down_step, 0)


def mlp_weights(where, z_sets, d_sets, gain, w_up, w_down, layer, before):
    hi, half, width = z_sets[0].shape
    lo = 2
    rows = hi * lo * 2 * half
    layers, _, hid = w_up.shape
    tile = 256
    flops = 3 * 2 * 4 * rows * width * hid
    call = pl.pallas_call(
        functools.partial(mlp_weights_kernel, hi, lo, half),
        grid=(hid // tile,),
        in_specs=[pl.BlockSpec(memory_space=pltpu.SMEM)]
        + [pl.BlockSpec(memory_space=pl.ANY)] * 8
        + [
            pl.BlockSpec((1, width), lambda j: (0, 0)),
            pl.BlockSpec((None, width, tile), lambda j: (layer, 0, j)),
            pl.BlockSpec((None, tile, width), lambda j: (layer, j, 0)),
        ]
        + [pl.BlockSpec(memory_space=pl.ANY)] * len(before),
        out_specs=[
            pl.BlockSpec((None, width, tile), lambda j: (layer, 0, j)),
            pl.BlockSpec((None, tile, width), lambda j: (layer, j, 0)),
        ],
        out_shape=[
            jax.ShapeDtypeStruct((layers, width, hid), F32),
            jax.ShapeDtypeStruct((layers, hid, width), F32),
        ],
        input_output_aliases={12 + i: i for i in range(len(before))},
        scratch_shapes=[
            pltpu.VMEM((rows, width), F32),
            pltpu.VMEM((rows, width), F32),
            pltpu.VMEM((2, rows, width), BF16),
            pltpu.VMEM((2, width, rows), BF16),
            pltpu.VMEM((2, rows, width), BF16),
            pltpu.VMEM((2, tile, rows), BF16),
            pltpu.VMEM((2, rows, tile), BF16),
            pltpu.SemaphoreType.DMA((2,)),
        ],
        compiler_params=pltpu.CompilerParams(vmem_limit_bytes=VMEM_BYTES),
        cost_estimate=pl.CostEstimate(
            flops=flops, bytes_accessed=4 * (2 * rows * width + 4 * width * hid), transcendentals=rows * hid
        ),
        name="mlp_weights",
    )
    return call(where, *z_sets, *d_sets, gain.reshape(1, width), w_up, w_down, *before)


def att_weights_kernel(hi, lo, half, *refs):
    where = refs[0]
    z_sets, d_sets = refs[1:5], refs[5:9]
    gain, w_qkv, w_out = refs[9:12]
    g_qkv, g_out, stage_z, stage_d, a, at, d2, qkv, do, mixt, sems = refs[-11:]
    rows = stage_z.shape[0]
    image_rows = 2 * half
    cols = w_out.shape[0]
    step = 256
    load_rows(where, z_sets, d_sets, gain, hi, lo, half, stage_z, stage_d, a, at, d2, sems)
    for part in range(3):
        w = cut(w_qkv[part])

        def in_step(i, carry, part=part, w=w):
            r = pl.ds(pl.multiple_of(i * step, step), step)
            qkv[part, r, :] = mul3((a[0, r, :], a[1, r, :]), w, NN)
            return carry

        lax.fori_loop(0, rows // step, in_step, 0)
    wo = cut(w_out[...])

    def do_step(i, carry):
        r = pl.ds(pl.multiple_of(i * step, step), step)
        do[r, :] = mul3((d2[0, r, :], d2[1, r, :]), wo, NT)
        return carry

    lax.fori_loop(0, rows // step, do_step, 0)
    masks = head_masks(cols, HEAD)

    def image_step(i, carry):
        r = pl.ds(pl.multiple_of(i * image_rows, image_rows), image_rows)
        mix, dq, dk, dv = attend_back(qkv[0, r, :], qkv[1, r, :], qkv[2, r, :], do[r, :], masks, HEAD)
        qkv[0, r, :] = dq
        qkv[1, r, :] = dk
        qkv[2, r, :] = dv
        mixt[0, :, r], mixt[1, :, r] = cut(mix.T)
        return carry

    lax.fori_loop(0, hi * lo, image_step, 0)
    width = stage_z.shape[1]
    for part in range(3):
        g = cut(qkv[part])

        def up_step(i, carry, part=part, g=g):
            r = pl.ds(pl.multiple_of(i * step, step), step)
            g_qkv[part, r, :] = mul3((at[0, r, :], at[1, r, :]), g, NN)
            return carry

        lax.fori_loop(0, width // step, up_step, 0)
    mt = (mixt[0], mixt[1])

    def out_step(i, carry):
        r = pl.ds(pl.multiple_of(i * step, step), step)
        g_out[:, r] = mul3(mt, (d2[0, :, r], d2[1, :, r]), NN)
        return carry

    lax.fori_loop(0, width // step, out_step, 0)


def att_weights(where, z_sets, d_sets, gain, w_qkv, w_out, layer, before):
    hi, half, width = z_sets[0].shape
    lo = 2
    rows = hi * lo * 2 * half
    layers, cols, _ = w_out.shape
    flops = 3 * 2 * 8 * rows * width * cols
    call = pl.pallas_call(
        functools.partial(att_weights_kernel, hi, lo, half),
        grid=(1,),
        in_specs=[pl.BlockSpec(memory_space=pltpu.SMEM)]
        + [pl.BlockSpec(memory_space=pl.ANY)] * 8
        + [
            pl.BlockSpec((1, width), lambda j: (0, 0)),
            pl.BlockSpec((None, 3, width, cols), lambda j: (layer, 0, 0, 0)),
            pl.BlockSpec((None, cols, width), lambda j: (layer, 0, 0)),
        ]
        + [pl.BlockSpec(memory_space=pl.ANY)] * len(before),
        out_specs=[
            pl.BlockSpec((None, 3, width, cols), lambda j: (layer, 0, 0, 0)),
            pl.BlockSpec((None, cols, width), lambda j: (layer, 0, 0)),
        ],
        out_shape=[
            jax.ShapeDtypeStruct((layers, 3, width, cols), F32),
            jax.ShapeDtypeStruct((layers, cols, width), F32),
        ],
        input_output_aliases={12 + i: i for i in range(len(before))},
        scratch_shapes=[
            pltpu.VMEM((rows, width), F32),
            pltpu.VMEM((rows, width), F32),
            pltpu.VMEM((2, rows, width), BF16),
            pltpu.VMEM((2, width, rows), BF16),
            pltpu.VMEM((2, rows, width), BF16),
            pltpu.VMEM((3, rows, cols), F32),
            pltpu.VMEM((rows, cols), F32),
            pltpu.VMEM((2, cols, rows), BF16),
            pltpu.SemaphoreType.DMA((2,)),
        ],
        compiler_params=pltpu.CompilerParams(vmem_limit_bytes=VMEM_BYTES),
        cost_estimate=pl.CostEstimate(
            flops=flops, bytes_accessed=4 * (2 * rows * width + 8 * width * cols), transcendentals=rows * 512
        ),
        name="att_weights",
    )
    return call(where, *z_sets, *d_sets, gain.reshape(1, width), w_qkv, w_out, *before)


def put_halves(core, mine, other, full):
    half = mine.shape[0]
    full[pl.ds(pl.multiple_of(core * half, half), half), :] = mine[...]
    full[pl.ds(pl.multiple_of((1 - core) * half, half), half), :] = other[...]


def get_halves(core, full, mine, other):
    half = mine.shape[0]
    mine[...] = full[pl.ds(pl.multiple_of(core * half, half), half), :]
    if other is not None:
        other[...] = full[pl.ds(pl.multiple_of((1 - core) * half, half), half), :]


def mul3_few(left, right, dims):
    rows = left[0].shape[0]
    one = functools.partial(lax.dot_general, dimension_numbers=dims, preferred_element_type=F32)
    both = one(jnp.concatenate([left[0], left[1]], axis=0), right[0])
    return (both[:rows] + both[rows:]) + one(left[0], right[1])


def mlp_forward_kernel(where, z_ref, w_ref, wo_ref, gain, w_up, w_down,
                       z_out, z_half, pre_out, mine, other, a, acc):
    core = where[2]
    j = pl.program_id(0)

    @pl.when(j == 0)
    def _():
        put_halves(core, w_ref, wo_ref, acc)
        z_new = z_ref[...] + acc[...]
        z_out[...] = z_new
        a[0], a[1] = cut(normed(z_new)[0] * gain[...])
        get_halves(core, z_out, z_half, None)
        acc[...] = jnp.zeros_like(acc)

    pre = mul3_few((a[0], a[1]), cut(w_up[...]), NN)
    pre_out[...] = pre
    hidden, _ = gelu_parts(pre)
    acc[...] += mul3_few(cut(hidden), cut(w_down[...]), NN)

    @pl.when(j == pl.num_programs(0) - 1)
    def _():
        get_halves(core, acc, mine, other)


def mlp_forward(where, z, w, wo, gain, w_up, w_down, layer):
    rows, width = z.shape
    half = rows // 2
    hid = w_up.shape[2]
    tile = 256
    whole = lambda shape: pl.BlockSpec(shape, lambda j: (0, 0))
    return pl.pallas_call(
        mlp_forward_kernel,
        grid=(hid // tile,),
        in_specs=[
            pl.BlockSpec(memory_space=pltpu.SMEM),
            whole((rows, width)),
            whole((half, width)),
            whole((half, width)),
            whole((1, width)),
            pl.BlockSpec((None, width, tile), lambda j: (layer, 0, j)),
            pl.BlockSpec((None, tile, width), lambda j: (layer, j, 0)),
        ],
        out_specs=[
            whole((rows, width)),
            whole((half, width)),
            pl.BlockSpec((rows, tile), lambda j: (0, j)),
            whole((half, width)),
            whole((half, width)),
        ],
        out_shape=[
            jax.ShapeDtypeStruct((rows, width), F32),
            jax.ShapeDtypeStruct((half, width), F32),
            jax.ShapeDtypeStruct((rows, hid), F32),
            jax.ShapeDtypeStruct((half, width), F32),
            jax.ShapeDtypeStruct((half, width), F32),
        ],
        scratch_shapes=[pltpu.VMEM((2, rows, width), BF16), pltpu.VMEM((rows, width), F32)],
        compiler_params=pltpu.CompilerParams(vmem_limit_bytes=VMEM_BYTES // 2),
        cost_estimate=pl.CostEstimate(
            flops=3 * 4 * rows * width * hid, bytes_accessed=8 * width * hid, transcendentals=rows * hid
        ),
        name="mlp_forward",
    )(where, z, w, wo, gain.reshape(1, width), w_up, w_down)


def att_forward_kernel(where, z_ref, w_ref, wo_ref, gain, w_qkv, w_out,
                       z_out, z_half, qkv_out, mine, other, acc):
    core = where[2]
    put_halves(core, w_ref, wo_ref, acc)
    z_new = z_ref[...] + acc[...]
    z_out[...] = z_new
    get_halves(core, z_out, z_half, None)
    a = cut(normed(z_new)[0] * gain[...])
    parts = []
    for part in range(3):
        one = mul3_few(a, cut(w_qkv[part]), NN)
        qkv_out[part] = one
        parts.append(one)
    masks = head_masks(w_out.shape[0], HEAD)
    mix, _, _ = attend(*parts, masks, HEAD)
    acc[...] = mul3_few(cut(mix), cut(w_out[...]), NN)
    get_halves(core, acc, mine, other)


def att_forward(where, z, w, wo, gain, w_qkv, w_out):
    rows, width = z.shape
    half = rows // 2
    cols = w_out.shape[0]
    vm = pl.BlockSpec(memory_space=pltpu.VMEM)
    return pl.pallas_call(
        att_forward_kernel,
        in_specs=[pl.BlockSpec(memory_space=pltpu.SMEM)] + [vm] * 6,
        out_specs=[vm] * 5,
        out_shape=[
            jax.ShapeDtypeStruct((rows, width), F32),
            jax.ShapeDtypeStruct((half, width), F32),
            jax.ShapeDtypeStruct((3, rows, cols), F32),
            jax.ShapeDtypeStruct((half, width), F32),
            jax.ShapeDtypeStruct((half, width), F32),
        ],
        scratch_shapes=[pltpu.VMEM((rows, width), F32)],
        compiler_params=pltpu.CompilerParams(vmem_limit_bytes=VMEM_BYTES // 2),
        cost_estimate=pl.CostEstimate(
            flops=3 * 8 * rows * width * cols, bytes_accessed=16 * width * cols, transcendentals=rows * 512
        ),
        name="att_forward",
    )(where, z, w, wo, gain.reshape(1, width), w_qkv, w_out)


def add_norm_back(core, d_ref, w_ref, wo_ref, z_ref, gain, d_out, d_half, g_out, acc):
    put_halves(core, w_ref, wo_ref, acc)
    dv, dg = norm_back(acc[...], z_ref[...], gain[...])
    g_out[...] = dg
    d_out[...] = d_ref[...] + dv
    get_halves(core, d_out, d_half, None)


def mlp_backward_kernel(where, d_ref, w_ref, wo_ref, z_ref, gain, pre, w_up, w_down,
                        d_out, d_half, g_out, mine, other, d2, acc):
    core = where[2]
    j = pl.program_id(0)

    @pl.when(j == 0)
    def _():
        add_norm_back(core, d_ref, w_ref, wo_ref, z_ref, gain, d_out, d_half, g_out, acc)
        d2[0], d2[1] = cut(d_out[...])
        acc[...] = jnp.zeros_like(acc)

    _, slope = gelu_parts(pre[...])
    du = mul3_few((d2[0], d2[1]), cut(w_down[...]), NT) * slope
    acc[...] += mul3_few(cut(du), cut(w_up[...]), NT)

    @pl.when(j == pl.num_programs(0) - 1)
    def _():
        get_halves(core, acc, mine, other)


def mlp_backward(where, d, w, wo, z_prev, gain_prev, pre, w_up, w_down, layer):
    rows, width = d.shape
    half = rows // 2
    hid = w_up.shape[2]
    tile = 256
    whole = lambda shape: pl.BlockSpec(shape, lambda j: (0, 0))
    return pl.pallas_call(
        mlp_backward_kernel,
        grid=(hid // tile,),
        in_specs=[
            pl.BlockSpec(memory_space=pltpu.SMEM),
            whole((rows, width)),
            whole((half, width)),
            whole((half, width)),
            whole((rows, width)),
            whole((1, width)),
            pl.BlockSpec((rows, tile), lambda j: (0, j)),
            pl.BlockSpec((None, width, tile), lambda j: (layer, 0, j)),
            pl.BlockSpec((None, tile, width), lambda j: (layer, j, 0)),
        ],
        out_specs=[
            whole((rows, width)),
            whole((half, width)),
            whole((1, width)),
            whole((half, width)),
            whole((half, width)),
        ],
        out_shape=[
            jax.ShapeDtypeStruct((rows, width), F32),
            jax.ShapeDtypeStruct((half, width), F32),
            jax.ShapeDtypeStruct((1, width), F32),
            jax.ShapeDtypeStruct((half, width), F32),
            jax.ShapeDtypeStruct((half, width), F32),
        ],
        scratch_shapes=[pltpu.VMEM((2, rows, width), BF16), pltpu.VMEM((rows, width), F32)],
        compiler_params=pltpu.CompilerParams(vmem_limit_bytes=VMEM_BYTES // 2),
        cost_estimate=pl.CostEstimate(
            flops=3 * 4 * rows * width * hid, bytes_accessed=8 * width * hid, transcendentals=rows * hid
        ),
        name="mlp_backward",
    )(where, d, w, wo, z_prev, gain_prev.reshape(1, width), pre, w_up, w_down)


def att_backward_kernel(where, d_ref, w_ref, wo_ref, z_ref, gain, qkv, w_qkv, w_out,
                        d_out, d_half, g_out, mine, other, acc):
    core = where[2]
    add_norm_back(core, d_ref, w_ref, wo_ref, z_ref, gain, d_out, d_half, g_out, acc)
    do = mul3_few(cut(d_out[...]), cut(w_out[...]), NT)
    masks = head_masks(w_out.shape[0], HEAD)
    _, dq, dk, dv = attend_back(qkv[0], qkv[1], qkv[2], do, masks, HEAD)
    acc[...] = mul3_few(cut(dq), cut(w_qkv[0]), NT)
    acc[...] += mul3_few(cut(dk), cut(w_qkv[1]), NT)
    acc[...] += mul3_few(cut(dv), cut(w_qkv[2]), NT)
    get_halves(core, acc, mine, other)


def att_backward(where, d, w, wo, z_prev, gain_prev, qkv, w_qkv, w_out):
    rows, width = d.shape
    half = rows // 2
    cols = w_out.shape[0]
    vm = pl.BlockSpec(memory_space=pltpu.VMEM)
    return pl.pallas_call(
        att_backward_kernel,
        in_specs=[pl.BlockSpec(memory_space=pltpu.SMEM)] + [vm] * 8,
        out_specs=[vm] * 5,
        out_shape=[
            jax.ShapeDtypeStruct((rows, width), F32),
            jax.ShapeDtypeStruct((half, width), F32),
            jax.ShapeDtypeStruct((1, width), F32),
            jax.ShapeDtypeStruct((half, width), F32),
            jax.ShapeDtypeStruct((half, width), F32),
        ],
        scratch_shapes=[pltpu.VMEM((rows, width), F32)],
        compiler_params=pltpu.CompilerParams(vmem_limit_bytes=VMEM_BYTES // 2),
        cost_estimate=pl.CostEstimate(
            flops=3 * 8 * rows * width * cols, bytes_accessed=16 * width * cols, transcendentals=rows * 512
        ),
        name="att_backward",
    )(where, d, w, wo, z_prev, gain_prev.reshape(1, width), qkv, w_qkv, w_out)


MASK_FILL = -1000000000.0
PRECISE = lax.Precision.HIGH
HEADS = 16


def layer_norm(values, gain_vec):
    centre = jnp.mean(values, axis=-1, keepdims=True)
    centred = values - centre
    spread = jnp.mean(centred * centred, axis=-1, keepdims=True)
    return centred * lax.rsqrt(spread + EPSILON) * gain_vec


def product(left_side, right_side):
    return jnp.dot(left_side, right_side, precision=PRECISE)


def contract_rows(left_side, right_side):
    return lax.dot_general(left_side, right_side, (((0,), (0,)), ((), ())), precision=PRECISE)


def contract_last(left_side, right_side):
    return lax.dot_general(left_side, right_side, (((1,), (1,)), ((), ())), precision=PRECISE)


def attention(queries, keys_in, values_in, key_bias, images, head_width):
    query_len = queries.shape[0] // images
    key_len = keys_in.shape[0] // images
    head_count = queries.shape[1] // head_width
    query_heads = queries.reshape(images, query_len, head_count, head_width)
    key_heads = keys_in.reshape(images, key_len, head_count, head_width)
    value_heads = values_in.reshape(images, key_len, head_count, head_width)
    scores = jnp.einsum("bqhd,bkhd->bhqk", query_heads, key_heads, precision=PRECISE)
    scores = scores / math.sqrt(head_width)
    if key_bias is not None:
        scores = scores + key_bias[:, None, None, :]
    weights = jax.nn.softmax(scores, axis=-1)
    mixture = jnp.einsum("bhqk,bkhd->bqhd", weights, value_heads, precision=PRECISE)
    return mixture.reshape(images * query_len, head_count * head_width)


def gelu_pair(pre):
    return jax.vjp(jax.nn.gelu, pre)


def make_body(dp, mp):
    ny = mp // 2
    lo = 2
    hi = dp // lo

    def mp_perm(fn):
        return [(i, fn(i)) for i in range(mp)]

    def core_swap(piece):
        return lax.ppermute(piece, "mp", mp_perm(lambda i: i ^ 1))

    def y_shift(piece, step):
        return lax.ppermute(piece, "mp", mp_perm(lambda i: (i + 2 * step) % mp))

    def core_idx():
        return lax.axis_index("mp") % 2

    def by_core(first, second, axis):
        core = core_idx()
        return jnp.where(
            core == 0,
            jnp.concatenate([first, second], axis),
            jnp.concatenate([second, first], axis),
        )

    def halves(partial):
        half = partial.shape[0] // 2
        core = core_idx()
        return (
            lax.dynamic_slice_in_dim(partial, core * half, half, 0),
            lax.dynamic_slice_in_dim(partial, (1 - core) * half, half, 0),
        )

    def sum_halves(mine, other):
        total = mine + core_swap(other)
        whole = total
        for step in range(1, ny):
            whole = whole + y_shift(total, step)
        return whole, core_swap(whole)

    def sum_rows(partial):
        rows = partial.shape[0] // mp
        core = core_idx()
        y_idx = lax.axis_index("mp") // 2
        blocks = partial.reshape(ny, 2, rows, partial.shape[1])
        mine = lax.dynamic_index_in_dim(blocks, core, 1, keepdims=False)
        other = lax.dynamic_index_in_dim(blocks, 1 - core, 1, keepdims=False)
        total = mine + core_swap(other)
        whole = lax.dynamic_index_in_dim(total, y_idx, 0, keepdims=False)
        for step in range(1, ny):
            away = lax.dynamic_index_in_dim(total, (y_idx + step) % ny, 0, keepdims=False)
            whole = whole + y_shift(away, step)
        return whole

    def gather_rows(piece):
        y_idx = lax.axis_index("mp") // 2
        if ny == 2:
            away = y_shift(piece, 1)
            column = jnp.where(
                y_idx == 0, jnp.stack([piece, away]), jnp.stack([away, piece])
            )
        else:
            column = jnp.zeros((ny,) + piece.shape, piece.dtype)
            column = lax.dynamic_update_index_in_dim(column, piece, y_idx, 0)
            for step in range(1, ny):
                away = y_shift(piece, step)
                column = lax.dynamic_update_index_in_dim(column, away, (y_idx - step) % ny, 0)
        both = by_core(column[:, None], core_swap(column)[:, None], 1)
        return both.reshape(mp * piece.shape[0], piece.shape[1])

    def gather_images(half):
        pieces = [half]
        for step in range(1, hi):
            pieces.append(lax.ppermute(half, "dp", [(i, (i - lo * step) % dp) for i in range(dp)]))
        column = jnp.stack(pieces)
        away = lax.ppermute(column, "dp", [(i, i ^ 1) for i in range(dp)])
        return column, away, core_swap(column), core_swap(away)

    def body(
        interface,
        latents,
        keep_mask,
        read_gain_lat,
        read_gain_int,
        read_query,
        read_keyval,
        read_out,
        read_gain_mlp,
        read_up,
        read_down,
        self_gain_att,
        self_qkv,
        self_out,
        self_gain_mlp,
        self_up,
        self_down,
        write_gain_int,
        write_gain_lat,
        write_query,
        write_keyval,
        write_out,
        write_gain_mlp,
        write_up,
        write_down,
        grad_interface_out,
        grad_latents_out,
    ):
        images = keep_mask.shape[0]
        layers = self_up.shape[0]
        shard_rows = interface.shape[0]
        lat_rows = latents.shape[0]
        latent_head = latents.shape[1] // HEADS
        patch_head = interface.shape[1] // HEADS
        own_rows = mp * lat_rows // images
        all_rows = dp * mp * lat_rows
        everywhere = images == 1 and dp % 2 == 0 and all_rows <= 2048
        mp_idx = lax.axis_index("mp")

        def spread(half):
            return gather_images(half) if everywhere else None

        def slow_mlp_weights(z, d, gain, w_up, w_down):
            n = layer_norm(z, gain)
            hidden, pull = gelu_pair(product(n, w_up))
            (du,) = pull(contract_last(d, w_down))
            return lax.psum((contract_rows(n, du), contract_rows(hidden, d)), "dp")

        def slow_att_weights(z, d, gain, w_qkv, w_out):
            n = layer_norm(z, gain)
            mix, back = jax.vjp(lambda *w: attend_self(n, *w), w_qkv[0], w_qkv[1], w_qkv[2])
            three = back(contract_last(d, w_out))
            return lax.psum((jnp.stack(three), contract_rows(mix, d)), "dp")

        def own_latents(block):
            return lax.dynamic_slice_in_dim(block, mp_idx * lat_rows, lat_rows, 0)

        flat_keep = keep_mask.reshape(-1).astype(jnp.float32)
        keep_rows = lax.dynamic_slice_in_dim(flat_keep, mp_idx * shard_rows, shard_rows, 0)[:, None]
        read_bias = jnp.where(keep_mask > 0, 0.0, MASK_FILL).astype(jnp.float32)

        def attend_read(qn, kn, wq, wk, wv):
            return attention(product(qn, wq), product(kn, wk), product(kn, wv), read_bias, images, latent_head)

        def attend_self(n, wq, wk, wv):
            return attention(product(n, wq), product(n, wk), product(n, wv), None, n.shape[0] // own_rows, latent_head)

        def attend_write(qn, m, wq, wk, wv):
            return attention(product(qn, wq), product(m, wk), product(m, wv), None, images, patch_head)

        x0 = interface * keep_rows
        z0 = gather_rows(latents)
        x0_full = gather_rows(x0)
        x0_read = layer_norm(x0_full, read_gain_int)
        z0_norm = layer_norm(z0, read_gain_lat)
        mix_read, back_read = jax.vjp(
            attend_read, z0_norm, x0_read, read_query, read_keyval[0], read_keyval[1]
        )
        dp_idx = lax.axis_index("dp")
        where = jnp.stack([dp_idx // lo, dp_idx % lo, core_idx()]).astype(jnp.int32)
        read_up3, read_down3 = read_up[None], read_down[None]
        sums = sum_halves(*halves(product(mix_read, read_out)))
        z1, z1_half, pre_read, *parts = mlp_forward(
            where, z0, *sums, read_gain_mlp, read_up3, read_down3, 0
        )
        z1_sets = spread(z1_half)
        sums = sum_halves(*parts)
        z = z1
        kept = []
        for layer in range(layers):
            z_in, in_half, qkv, *parts = att_forward(
                where, z, *sums, self_gain_att[layer], self_qkv[layer], self_out[layer]
            )
            in_sets = spread(in_half)
            sums = sum_halves(*parts)
            z_mid, mid_half, pre, *parts = mlp_forward(
                where, z_in, *sums, self_gain_mlp[layer], self_up, self_down, layer
            )
            mid_sets = spread(mid_half)
            sums = sum_halves(*parts)
            kept.append((z_in, in_sets, qkv, z_mid, mid_sets, pre))
            z = z_mid
        z_out = z + by_core(*sums, 0)

        x0_write = layer_norm(x0_full, write_gain_int)
        m_norm = layer_norm(z_out, write_gain_lat)
        mix_write, back_write = jax.vjp(
            attend_write, x0_write, m_norm, write_query, write_keyval[0], write_keyval[1]
        )
        x1 = x0 + sum_rows(product(mix_write, write_out))
        x1_norm = gather_rows(layer_norm(x1, write_gain_mlp))
        hidden_w, pull_w = gelu_pair(product(x1_norm, write_up))
        interface_out = x1 + sum_rows(product(hidden_w, write_down))

        gx_full = gather_rows(grad_interface_out)
        (du_w,) = pull_w(contract_last(gx_full, write_down))
        dn_w = sum_rows(contract_last(du_w, write_up))
        _, pull_norm = jax.vjp(layer_norm, x1, write_gain_mlp)
        dx_norm, gain_write_mlp = pull_norm(dn_w)
        gx1 = grad_interface_out + dx_norm
        gx1_full = gather_rows(gx1)
        pulled = back_write(contract_last(gx1_full, write_out))
        sums = sum_halves(*halves(pulled[1]))
        dq_rows = sum_rows(pulled[0])
        _, pull_norm = jax.vjp(layer_norm, x0, write_gain_int)
        dx_q, gain_write_int = pull_norm(dq_rows)
        grad_x = gx1 + dx_q
        grads_write = lax.psum(
            (
                pulled[2],
                jnp.stack([pulled[3], pulled[4]]),
                contract_rows(mix_write, gx1_full),
                contract_rows(x1_norm, du_w),
                contract_rows(hidden_w, gx_full),
            ),
            "dp",
        )

        d = gather_rows(grad_latents_out)
        prev, prev_gain = z_out, write_gain_lat
        gains_att = [None] * layers
        gains_mlp = [None] * layers
        before_mlp = before_att = ()
        slow_mlp = [None] * layers
        slow_att = [None] * layers
        for layer in reversed(range(layers)):
            z_in, in_sets, qkv, z_mid, mid_sets, pre = kept[layer]
            d, d_half, gain, *parts = mlp_backward(
                where, d, *sums, prev, prev_gain, pre, self_up, self_down, layer
            )
            if layer == layers - 1:
                gain_write_lat = gain[0]
            else:
                gains_att[layer + 1] = gain[0]
            sums = sum_halves(*parts)
            d_sets = spread(d_half)
            if everywhere:
                before_mlp = mlp_weights(
                    where, mid_sets, d_sets, self_gain_mlp[layer], self_up, self_down, layer, before_mlp
                )
            else:
                slow_mlp[layer] = slow_mlp_weights(
                    z_mid, d, self_gain_mlp[layer], self_up[layer], self_down[layer]
                )
            d, d_half, gain, *parts = att_backward(
                where, d, *sums, z_mid, self_gain_mlp[layer], qkv, self_qkv[layer], self_out[layer]
            )
            gains_mlp[layer] = gain[0]
            sums = sum_halves(*parts)
            d_sets = spread(d_half)
            if everywhere:
                before_att = att_weights(
                    where, in_sets, d_sets, self_gain_att[layer], self_qkv, self_out, layer, before_att
                )
            else:
                slow_att[layer] = slow_att_weights(
                    z_in, d, self_gain_att[layer], self_qkv[layer], self_out[layer]
                )
            prev, prev_gain = z_in, self_gain_att[layer]
        d, d_half, gain, *parts = mlp_backward(
            where, d, *sums, prev, prev_gain, pre_read, read_up3, read_down3, 0
        )
        gains_att[0] = gain[0]
        sums = sum_halves(*parts)
        if everywhere:
            d_sets = spread(d_half)
            grad_read_up, grad_read_down = (
                one[0]
                for one in mlp_weights(
                    where, z1_sets, d_sets, read_gain_mlp, read_up3, read_down3, 0, ()
                )
            )
            self_up_grad, self_down_grad = before_mlp
            self_qkv_grad, self_out_grad = before_att
        else:
            grad_read_up, grad_read_down = slow_mlp_weights(
                z1, d, read_gain_mlp, read_up, read_down
            )
            self_up_grad = jnp.stack([one[0] for one in slow_mlp])
            self_down_grad = jnp.stack([one[1] for one in slow_mlp])
            self_qkv_grad = jnp.stack([one[0] for one in slow_att])
            self_out_grad = jnp.stack([one[1] for one in slow_att])

        _, pull_norm = jax.vjp(layer_norm, z1, read_gain_mlp)
        dz_norm, gain_read_mlp = pull_norm(by_core(*sums, 0))
        d = d + dz_norm
        pulled = back_read(contract_last(d, read_out))
        dn_lat = sum_rows(pulled[0])
        _, pull_norm = jax.vjp(layer_norm, latents, read_gain_lat)
        dz_lat, gain_read_lat = pull_norm(dn_lat)
        grad_latents = own_latents(d) + dz_lat
        dn_int = sum_rows(pulled[1])
        _, pull_norm = jax.vjp(layer_norm, x0, read_gain_int)
        dx_k, gain_read_int = pull_norm(dn_int)
        grad_interface = (grad_x + dx_k) * keep_rows
        grads_write, d = lax.optimization_barrier((grads_write, d))
        grads_read = lax.psum(
            (pulled[2], jnp.stack([pulled[3], pulled[4]]), contract_rows(mix_read, d)), "dp"
        )

        once = (mp_idx == 0).astype(jnp.float32)
        gains = lax.psum(
            (
                gain_read_lat,
                gain_read_int,
                gain_read_mlp * once,
                jnp.stack(gains_att) * once,
                jnp.stack(gains_mlp) * once,
                gain_write_int,
                gain_write_lat * once,
                gain_write_mlp,
            ),
            ("dp", "mp"),
        )
        return (
            interface_out,
            own_latents(z_out),
            grad_interface,
            grad_latents,
            gains[0],
            gains[1],
            grads_read[0],
            grads_read[1],
            grads_read[2],
            gains[2],
            grad_read_up,
            grad_read_down,
            gains[3],
            self_qkv_grad,
            self_out_grad,
            gains[4],
            self_up_grad,
            self_down_grad,
            gains[5],
            gains[6],
            grads_write[0],
            grads_write[1],
            grads_write[2],
            gains[7],
            grads_write[3],
            grads_write[4],
        )

    return body


def solution(mesh):
    rows = P(("dp", "mp"), None)
    columns = P(None, "mp")
    heads_in = P("mp", None)
    in_specs = (
        rows,
        rows,
        P("dp", None),
        P(),
        P(),
        columns,
        P(None, None, "mp"),
        heads_in,
        P(),
        columns,
        heads_in,
        P(),
        P(None, None, None, "mp"),
        P(None, "mp", None),
        P(),
        P(None, None, "mp"),
        P(None, "mp", None),
        P(),
        P(),
        columns,
        P(None, None, "mp"),
        heads_in,
        P(),
        columns,
        heads_in,
        rows,
        rows,
    )
    out_specs = (rows, rows, rows, rows) + in_specs[3:25]
    body = make_body(mesh.shape["dp"], mesh.shape["mp"])
    return jax.shard_map(body, mesh=mesh, in_specs=in_specs, out_specs=out_specs, check_vma=False)
```

time: 2220 us -> 991 us (0.45)
  waiting for transfers between devices: 1610 us -> 276 us
  Pallas kernels: 0 us -> 297 us
  matrix products: 284 us -> 65.5 us
  starting transfers between devices: 1.59 us -> 144 us
  blocking collectives: 142 us -> 41.1 us
    psum x1 -> x2, waiting for transfers between devices: 1220 us -> 0.02 us  [body(): lax.psum((pulled[2], jnp.stack([pulled[3], pulled[4]]), contract_rows(mix...]
    reduce_scatter x18 -> x0, waiting for transfers between devices: 322 us -> none  [the longest x8 169 us: branch_sum(): lax.psum_scatter(product(source, weight), 'mp', scatter_dimension=0, tile...]
    pallas_call x0 -> x15, Pallas kernels: none -> 297 us  [the longest x3 146 us: mlp_weights(): call(where, *z_sets, *d_sets, gain.reshape(1, width), w_up, w_down, *before)]
    ppermute x0 -> x120, waiting for transfers between devices: none -> 276 us  [the longest x24 124 us: y_shift(): return lax.ppermute(piece, 'mp', mp_perm(lambda i: (i + 2 * step) % mp))]
    dot_general x56 -> x22, matrix products: 186 us -> 32.3 us  [product(): return jnp.dot(left_side, right_side, precision=PRECISE)]
    ppermute x0 -> x120, starting transfers between devices: none -> 144 us  [the longest x30 100 us: gather_images(): lax.ppermute(half, 'dp', [(i, (i - lo * step) % dp) for i in range(dp)])]
    all_gather x13 -> x0, blocking collectives: 94.5 us -> none  [the longest x7 51.9 us: gather_rows(): return lax.all_gather(pieces_in, 'mp', axis=0, tiled=True)]
    all_gather x5 -> x0, waiting for transfers between devices: 69.7 us -> none  [the longest x2 42.8 us: spread_grad(): return lax.all_gather(grad_shard, 'mp', axis=0, tiled=True)]
  transfers between devices with their start and end apart: 24 -> 122, of which waited for: 20 -> 51; matrix products, arithmetic and copies ran while one was open for 8% -> 12% of each run, Pallas kernels for 0% -> 27%
where the time goes in v1:
time: 991 us; the launch traced here: 981 us
  Pallas kernels  297 us (30%)
  waiting for transfers between devices  276 us (28%)
  starting transfers between devices  144 us (15%)
  local copies, waits for them, and re-layouts  74.7 us (8%)
  other arithmetic  65.7 us (7%)
  matrix products  65.5 us (7%)
  blocking collectives  41.1 us (4%)
  between operations  17.6 us (2%)
    pallas_call x3, Pallas kernels, mlp_weights(): call(where, *z_sets, *d_sets, gain.reshape(1, width), w_up, w_down, *before)  146 us
    ppermute x24, waiting for transfers between devices, y_shift(): return lax.ppermute(piece, 'mp', mp_perm(lambda i: (i + 2 * step) % mp))  124 us
    ppermute x30, waiting for transfers between devices, gather_images(): lax.ppermute(half, 'dp', [(i, (i - lo * step) % dp) for i in range(dp)])  123 us
    ppermute x30, starting transfers between devices, gather_images(): lax.ppermute(half, 'dp', [(i, (i - lo * step) % dp) for i in range(dp)])  100 us
    pallas_call x2, Pallas kernels, att_weights(): call(where, *z_sets, *d_sets, gain.reshape(1, width), w_qkv, w_out, *before)  96.6 us
    unnamed x440, local copies, waits for them, and re-layouts  49.9 us
    psum x1, blocking collectives, body(): lax.psum((gain_read_lat, gain_read_int, gain_read_mlp * once, jnp.stack(g...  41.1 us
    dot_general x22, matrix products, product(): return jnp.dot(left_side, right_side, precision=PRECISE)  32.3 us
  transfers between devices with their start and end apart: 122, of which 51 were waited for; matrix products, arithmetic and copies ran while one was open for 12% of the time, Pallas kernels for 27%

profile of v1, /device:TPU:0, one launch (start us, length us, event | category | flops | bytes accessed | tf_op | source)
XLA Modules:
  0.0 981.4 jit_solution(17138668356542115260)
XLA Ops:
  21.1 5.2 collective-permute-done.2
  46.2 7.6 collective-permute-done.5
  59.8 5.8 mlp_forward.3
  68.9 4.1 slice_bitcast_fusion
  83.8 7.5 collective-permute-done.11
  93.0 5.6 mlp_forward.4
  101.2 7.5 collective-permute-done.14
  116.2 7.5 collective-permute-done.17
  125.4 6.0 mlp_forward.5
  165.4 12.1 %collective-permute-done.23 = f32[256,512]{1,0:T(8,128)} collective-permute-done((f32[256,512]{1,0:T(8,128)S(1)}, f32[256,512]{1,0:T(8,128)}, u32[]{:S(2)}, u32[]{:S(2)}) %collective-permute-start.23) | collective-permute-done | bytes 524320 | tf_op jit(solution)/shard_map/ppermute | solution.py:643
  181.5 7.3 collective-permute-done.28
  190.8 8.6 collective-permute-done.24
  216.3 11.5 %collective-permute-done.31 = f32[256,512]{1,0:T(8,128)S(1)} collective-permute-done((f32[256,512]{1,0:T(8,128)S(1)}, f32[256,512]{1,0:T(8,128)S(1)}, u32[]{:S(2)}, u32[]{:S(2)}) %collective-permute-start.31) | collective-permute-done | bytes 524320 | tf_op jit(solution)/shard_map/ppermute | solution.py:643
  228.6 9.8 %collective-permute-done.27 = f32[256,512]{1,0:T(8,128)S(1)} collective-permute-done((f32[256,512]{1,0:T(8,128)S(1)}, f32[256,512]{1,0:T(8,128)S(1)}, u32[]{:S(2)}, u32[]{:S(2)}) %collective-permute-start.27) | collective-permute-done | bytes 524320 | tf_op jit(solution)/shard_map/ppermute | solution.py:643
  241.5 12.5 %collective-permute-done.32 = f32[256,512]{1,0:T(8,128)S(1)} collective-permute-done((f32[256,512]{1,0:T(8,128)S(1)}, f32[256,512]{1,0:T(8,128)S(1)}, u32[]{:S(2)}, u32[]{:S(2)}) %collective-permute-start.32) | collective-permute-done | bytes 524320 | tf_op jit(solution)/shard_map/ppermute | solution.py:643
  270.0 9.0 collective-permute-done.36
  287.7 7.6 mlp_backward.3
  318.4 11.9 %collective-permute-start.73 = (f32[64,1024]{1,0:T(8,128)}, f32[64,1024]{1,0:T(8,128)S(1)}, u32[]{:S(2)}, u32[]{:S(2)}) collective-permute-start(f32[64,1024]{1,0:T(8,128)} %copy-done.43), channel_id=1, source_target_pairs={{0,16},{4,20},{8,24},{12,28},{16,0},{20,4},{24,8},{28,12},{1,17},{... | collective-permute-start | bytes 786440 | tf_op jit(solution)/shard_map/ppermute | solution.py:704
  330.4 14.9 %collective-permute-start.72 = (f32[64,1024]{1,0:T(8,128)}, f32[64,1024]{1,0:T(8,128)S(1)}, u32[]{:S(2)}, u32[]{:S(2)}) collective-permute-start(f32[64,1024]{1,0:T(8,128)} %copy-done.43), channel_id=1, source_target_pairs={{0,24},{4,28},{8,0},{12,4},{16,8},{20,12},{24,16},{28,20},{1,25},{... | collective-permute-start | bytes 786440 | tf_op jit(solution)/shard_map/ppermute | solution.py:704
  353.6 4.1 att_backward.2
  363.7 11.6 %collective-permute-start.85 = (f32[64,1024]{1,0:T(8,128)S(1)}, f32[64,1024]{1,0:T(8,128)S(1)}, u32[]{:S(2)}, u32[]{:S(2)}) collective-permute-start(f32[64,1024]{1,0:T(8,128)S(1)} %copy-done.48), channel_id=1, source_target_pairs={{0,16},{4,20},{8,24},{12,28},{16,0},{20,4},{24,8},{28,12},{1,17},{... | collective-permute-start | bytes 786440 | tf_op jit(solution)/shard_map/ppermute | solution.py:704
  375.3 9.7 collective-permute-done.97
  391.2 6.7 collective-permute-start.109
  399.4 8.2 collective-permute-done.85
  411.4 7.4 collective-permute-done.109
  426.5 6.9 mlp_backward.4
  437.4 6.1 collective-permute-start.116
  456.9 5.8 collective-permute-done.115
  471.7 4.6 att_backward.3
  477.6 4.2 collective-permute-start.92
  484.2 5.7 collective-permute-done.92
  492.2 8.6 collective-permute-done.91
  503.5 5.5 collective-permute-done.51
  515.5 6.8 mlp_backward.5
  525.3 4.2 collective-permute-start.104
  535.4 6.2 collective-permute-done.104
  541.6 21.2 %collective-permute-done.103 = f32[64,1024]{1,0:T(8,128)S(1)} collective-permute-done((f32[64,1024]{1,0:T(8,128)S(1)}, f32[64,1024]{1,0:T(8,128)S(1)}, u32[]{:S(2)}, u32[]{:S(2)}) %collective-permute-start.103) | collective-permute-done | bytes 262176 | tf_op jit(solution)/shard_map/ppermute | solution.py:704
  562.8 8.0 collective-permute-start.78
  575.3 32.8 %collective-permute-done.79 = f32[64,1024]{1,0:T(8,128)S(1)} collective-permute-done((f32[64,1024]{1,0:T(8,128)S(1)}, f32[64,1024]{1,0:T(8,128)S(1)}, u32[]{:S(2)}, u32[]{:S(2)}) %collective-permute-start.79) | collective-permute-done | bytes 262176 | tf_op jit(solution)/shard_map/ppermute | solution.py:704
  608.1 10.2 %collective-permute-done.78 = f32[64,1024]{1,0:T(8,128)S(1)} collective-permute-done((f32[64,1024]{1,0:T(8,128)S(1)}, f32[64,1024]{1,0:T(8,128)S(1)}, u32[]{:S(2)}, u32[]{:S(2)}) %collective-permute-start.78) | collective-permute-done | bytes 262176 | tf_op jit(solution)/shard_map/ppermute | solution.py:704
  618.8 48.7 %mlp_weights.4 = (f32[2,1024,1024]{2,1,0:T(8,128)}, f32[2,1024,1024]{2,1,0:T(8,128)}) custom-call(s32[3]{0:T(128)} %copy-done.58, f32[4,64,1024]{2,1,0:T(8,128)} %pad_maximum_fusion.10.refs_1_, f32[4,64,1024]{2,1,0:T(8,128)} %collective-permute-done.111.refs_2_, f32[4,64,1024]{2,1,0:T(8,128)} %copy-done.200, f32[4,64,1024]{2,1,0:T(8,128)} %copy-done.201, ...), custom_call_target="tpu_custom_call" | custom-call | flops 25769803776 | bytes 25165824 | tf_op jit(solution)/shard_map/mlp_weights/pallas_call | solution.py:241
  673.2 48.0 %att_weights.2 = (f32[2,3,1024,256]{3,2,1,0:T(8,128)}, f32[2,256,1024]{2,1,0:T(8,128)}) custom-call(s32[3]{0:T(128)} %copy-done.58, f32[4,64,1024]{2,1,0:T(8,128)} %pad_maximum_fusion.6.refs_1_, f32[4,64,1024]{2,1,0:T(8,128)} %collective-permute-done.87.refs_2_, f32[4,64,1024]{2,1,0:T(8,128)} %copy-done.204, f32[4,64,1024]{2,1,0:T(8,128)} %copy-done.205, ...), custom_call_target="tpu_custom_call" | custom-call | flops 12884901888 | bytes 16777216 | tf_op jit(solution)/shard_map/att_weights/pallas_call | solution.py:346
  757.7 48.8 %mlp_weights.5 = (f32[2,1024,1024]{2,1,0:T(8,128)}, f32[2,1024,1024]{2,1,0:T(8,128)}) custom-call(s32[3]{0:T(128)} %copy-done.58, f32[4,64,1024]{2,1,0:T(8,128)} %pad_maximum_fusion.8.refs_1_, f32[4,64,1024]{2,1,0:T(8,128)} %collective-permute-done.99.refs_2_, ...), custom_call_target="tpu_custom_call", output_to_operand_aliasing={{0}: (12, {}), {1}: (13, {})} | custom-call | flops 25769803776 | bytes 25165824 | tf_op jit(solution)/shard_map/mlp_weights/pallas_call | solution.py:241
  808.1 4.0 collective-permute-done.59
  812.4 4.5 collective-permute-done.81.refs_6_
  824.5 48.6 %att_weights.3 = (f32[2,3,1024,256]{3,2,1,0:T(8,128)}, f32[2,256,1024]{2,1,0:T(8,128)}) custom-call(s32[3]{0:T(128)} %copy-done.58, f32[4,64,1024]{2,1,0:T(8,128)} %pad_maximum_fusion.4.refs_1_, f32[4,64,1024]{2,1,0:T(8,128)} %collective-permute-done.75.refs_2_, f32[4,64,1024]{2,1,0:T(8,128)} %copy-done.202, ...), custom_call_target="tpu_custom_call", output_to_operand_aliasing={{0}: (12, {}), {1}: (13, {})} | custom-call | flops 12884901888 | bytes 16777216 | tf_op jit(solution)/shard_map/att_weights/pallas_call | solution.py:346
  874.2 41.1 %all-reduce = (f32[1024]{0:T(1024)}, f32[512]{0:T(512)}, f32[1024]{0:T(1024)}, f32[2,1024]{1,0:T(2,128)}, f32[2,1024]{1,0:T(2,128)}, /*index=5*/f32[512]{0:T(512)}, f32[1024]{0:T(1024)}, f32[512]{0:T(512)}) all-reduce(f32[1024]{0:T(1024)S(1)} %get-tuple-element.168, ...), channel_id=1, replica_groups=mesh['dp'=8,'mp'=4] {'dp','mp'}, use_global_device_ids=true, to_apply=%region_31.32 | all-reduce | flops 8704 | bytes 69632 | tf_op jit(solution)/shard_map/psum | solution.py:931
  916.7 48.7 %mlp_weights.3 = (f32[1,1024,1024]{2,1,0:T(8,128)}, f32[1,1024,1024]{2,1,0:T(8,128)}) custom-call(s32[3]{0:T(128)} %copy-done.58, f32[4,64,1024]{2,1,0:T(8,128)} %pad_maximum_fusion.2.refs_1_, f32[4,64,1024]{2,1,0:T(8,128)} %collective-permute-done.63.refs_2_, f32[4,64,1024]{2,1,0:T(8,128)} %collective-permute-done.64.refs_3_, ...), custom_call_target="tpu_custom_call" | custom-call | flops 25769803776 | bytes 25165824 | tf_op jit(solution)/shard_map/mlp_weights/pallas_call | solution.py:241
  (860 shorter events, 324.6 us)
Async XLA Ops:
  7.2 727.4 %all-reduce.8.cloned.1.call-start = ((), (), s32[]{:S(2)}) async-start(), calls=%async_computation.1 | async-start | bytes 7340032 | tf_op jit(solution)/shard_map/psum | solution.py:837
  311.3 34.0 %collective-permute-start.60 = (f32[64,1024]{1,0:T(8,128)}, f32[64,1024]{1,0:T(8,128)S(1)}, u32[]{:S(2)}, u32[]{:S(2)}) collective-permute-start(f32[64,1024]{1,0:T(8,128)} %copy-done.41), channel_id=1, source_target_pairs={{0,24},{4,28},{8,0},{12,4},{16,8},{20,12},{24,16},{28,20},{1,25},{... | collective-permute-start | bytes 786440 | tf_op jit(solution)/shard_map/ppermute | solution.py:704
  313.7 35.3 %collective-permute-start.43 = (f32[64,1024]{1,0:T(8,128)S(1)}, f32[64,1024]{1,0:T(8,128)S(1)}, u32[]{:S(2)}, u32[]{:S(2)}) collective-permute-start(f32[64,1024]{1,0:T(8,128)S(1)} %add.402.w_ref), channel_id=1, source_target_pairs={{0,1},{1,0},{2,3},{3,2},{4,5},{5,4},{6,7},{7,6},{8,9},{9,8},{10,11... | collective-permute-start | bytes 786440 | tf_op jit(solution)/shard_map/ppermute | solution.py:640
  315.7 42.8 %collective-permute-start.74 = (f32[64,1024]{1,0:T(8,128)}, f32[64,1024]{1,0:T(8,128)S(1)}, u32[]{:S(2)}, u32[]{:S(2)}) collective-permute-start(f32[64,1024]{1,0:T(8,128)} %copy-done.43), channel_id=1, source_target_pairs={{0,8},{4,12},{8,16},{12,20},{16,24},{20,28},{24,0},{28,4},{1,9},{5... | collective-permute-start | bytes 786440 | tf_op jit(solution)/shard_map/ppermute | solution.py:704
  318.4 44.1 %collective-permute-start.73 = (f32[64,1024]{1,0:T(8,128)}, f32[64,1024]{1,0:T(8,128)S(1)}, u32[]{:S(2)}, u32[]{:S(2)}) collective-permute-start(f32[64,1024]{1,0:T(8,128)} %copy-done.43), channel_id=1, source_target_pairs={{0,16},{4,20},{8,24},{12,28},{16,0},{20,4},{24,8},{28,12},{1,17},{... | collective-permute-start | bytes 786440 | tf_op jit(solution)/shard_map/ppermute | solution.py:704
  330.4 32.2 %collective-permute-start.72 = (f32[64,1024]{1,0:T(8,128)}, f32[64,1024]{1,0:T(8,128)S(1)}, u32[]{:S(2)}, u32[]{:S(2)}) collective-permute-start(f32[64,1024]{1,0:T(8,128)} %copy-done.43), channel_id=1, source_target_pairs={{0,24},{4,28},{8,0},{12,4},{16,8},{20,12},{24,16},{28,20},{1,25},{... | collective-permute-start | bytes 786440 | tf_op jit(solution)/shard_map/ppermute | solution.py:704
  349.0 36.0 %collective-permute-start.97 = (f32[64,1024]{1,0:T(8,128)}, f32[64,1024]{1,0:T(8,128)S(1)}, u32[]{:S(2)}, u32[]{:S(2)}) collective-permute-start(f32[64,1024]{1,0:T(8,128)} %copy-done.45), channel_id=1, source_target_pairs={{0,16},{4,20},{8,24},{12,28},{16,0},{20,4},{24,8},{28,12},{1,17},{... | collective-permute-start | bytes 786440 | tf_op jit(solution)/shard_map/ppermute | solution.py:704
  362.5 35.3 %collective-permute-start.44 = (f32[64,1024]{1,0:T(8,128)S(1)}, f32[64,1024]{1,0:T(8,128)S(1)}, u32[]{:S(2)}, u32[]{:S(2)}) collective-permute-start(f32[64,1024]{1,0:T(8,128)S(1)} %get-tuple-element.114), channel_id=1, source_target_pairs={{0,1},{1,0},{2,3},{3,2},{4,5},{5,4},{6,7},{7,6},{8,9},{9,8},{10,11... | collective-permute-start | bytes 786440 | tf_op jit(solution)/shard_map/ppermute | solution.py:640
  363.7 43.9 %collective-permute-start.85 = (f32[64,1024]{1,0:T(8,128)S(1)}, f32[64,1024]{1,0:T(8,128)S(1)}, u32[]{:S(2)}, u32[]{:S(2)}) collective-permute-start(f32[64,1024]{1,0:T(8,128)S(1)} %copy-done.48), channel_id=1, source_target_pairs={{0,16},{4,20},{8,24},{12,28},{16,0},{20,4},{24,8},{28,12},{1,17},{... | collective-permute-start | bytes 786440 | tf_op jit(solution)/shard_map/ppermute | solution.py:704
  409.8 67.7 %collective-permute-start.87 = (f32[4,64,1024]{2,1,0:T(8,128)}, f32[4,64,1024]{2,1,0:T(8,128)}, u32[]{:S(2)}, u32[]{:S(2)}) collective-permute-start(f32[4,64,1024]{2,1,0:T(8,128)} %pad_maximum_fusion.6.refs_1_), channel_id=1, source_target_pairs={{0,4},{4,0},{8,12},{12,8},{16,20},{20,16},{24,28},{28,24},{1,5},{5... | collective-permute-start | bytes 3145736 | tf_op jit(solution)/shard_map/ppermute | solution.py:706
  419.9 61.9 %collective-permute-start.111 = (f32[4,64,1024]{2,1,0:T(8,128)}, f32[4,64,1024]{2,1,0:T(8,128)}, u32[]{:S(2)}, u32[]{:S(2)}) collective-permute-start(f32[4,64,1024]{2,1,0:T(8,128)} %pad_maximum_fusion.10.refs_1_), channel_id=1, source_target_pairs={{0,4},{4,0},{8,12},{12,8},{16,20},{20,16},{24,28},{28,24},{1,5},{5... | collective-permute-start | bytes 3145736 | tf_op jit(solution)/shard_map/ppermute | solution.py:706
  462.7 48.1 %collective-permute-start.112 = (f32[4,64,1024]{2,1,0:T(8,128)}, f32[4,64,1024]{2,1,0:T(8,128)S(1)}, u32[]{:S(2)}, u32[]{:S(2)}) collective-permute-start(f32[4,64,1024]{2,1,0:T(8,128)} %pad_maximum_fusion.10.refs_1_), channel_id=1, source_target_pairs={{0,1},{1,0},{2,3},{3,2},{4,5},{5,4},{6,7},{7,6},{8,9},{9,8},{10,11... | collective-permute-start | bytes 3145736 | tf_op jit(solution)/shard_map/ppermute | solution.py:640
  466.8 45.6 %collective-permute-start.117 = (f32[4,64,1024]{2,1,0:T(8,128)}, f32[4,64,1024]{2,1,0:T(8,128)}, u32[]{:S(2)}, u32[]{:S(2)}) collective-permute-start(f32[4,64,1024]{2,1,0:T(8,128)} %pad_maximum_fusion.11.refs_5_), channel_id=1, source_target_pairs={{0,4},{4,0},{8,12},{12,8},{16,20},{20,16},{24,28},{28,24},{1,5},{5... | collective-permute-start | bytes 3145736 | tf_op jit(solution)/shard_map/ppermute | solution.py:706
  484.0 38.3 %collective-permute-start.113 = (f32[4,64,1024]{2,1,0:T(8,128)}, f32[4,64,1024]{2,1,0:T(8,128)S(1)}, u32[]{:S(2)}, u32[]{:S(2)}) collective-permute-start(f32[4,64,1024]{2,1,0:T(8,128)} %collective-permute-done.111.refs_2_), channel_id=1, source_target_pairs={{0,1},{1,0},{2,3},{3,2},{4,5},{5,4},{6,7},{7,6},{8,9},{9,8},{10,11... | collective-permute-start | bytes 3145736 | tf_op jit(solution)/shard_map/ppermute | solution.py:640
  510.8 60.0 %collective-permute-start.93 = (f32[4,64,1024]{2,1,0:T(8,128)}, f32[4,64,1024]{2,1,0:T(8,128)}, u32[]{:S(2)}, u32[]{:S(2)}) collective-permute-start(f32[4,64,1024]{2,1,0:T(8,128)} %pad_maximum_fusion.7.refs_5_), channel_id=1, source_target_pairs={{0,4},{4,0},{8,12},{12,8},{16,20},{20,16},{24,28},{28,24},{1,5},{5... | collective-permute-start | bytes 3145736 | tf_op jit(solution)/shard_map/ppermute | solution.py:706
  515.2 58.5 %collective-permute-start.119 = (f32[4,64,1024]{2,1,0:T(8,128)}, f32[4,64,1024]{2,1,0:T(8,128)}, u32[]{:S(2)}, u32[]{:S(2)}) collective-permute-start(f32[4,64,1024]{2,1,0:T(8,128)} %collective-permute-done.117.refs_6_), channel_id=1, source_target_pairs={{0,1},{1,0},{2,3},{3,2},{4,5},{5,4},{6,7},{7,6},{8,9},{9,8},{10,11... | collective-permute-start | bytes 3145736 | tf_op jit(solution)/shard_map/ppermute | solution.py:640
  524.4 441.0 %all-reduce.6.cloned.1.call-start = ((), (), s32[]{:S(2)}) async-start(), calls=%async_computation | async-start | bytes 6291456 | tf_op jit(solution)/shard_map/psum | solution.py:926
  529.5 33.3 %collective-permute-start.103 = (f32[64,1024]{1,0:T(8,128)S(1)}, f32[64,1024]{1,0:T(8,128)S(1)}, u32[]{:S(2)}, u32[]{:S(2)}) collective-permute-start(f32[64,1024]{1,0:T(8,128)S(1)} %copy-done.54), channel_id=1, source_target_pairs={{0,16},{4,20},{8,24},{12,28},{16,0},{20,4},{24,8},{28,12},{1,17},{... | collective-permute-start | bytes 786440 | tf_op jit(solution)/shard_map/ppermute | solution.py:704
  541.6 33.7 %collective-permute-start.80 = (f32[64,1024]{1,0:T(8,128)S(1)}, f32[64,1024]{1,0:T(8,128)S(1)}, u32[]{:S(2)}, u32[]{:S(2)}) collective-permute-start(f32[64,1024]{1,0:T(8,128)S(1)} %copy-done.56), channel_id=1, source_target_pairs={{0,8},{4,12},{8,16},{12,20},{16,24},{20,28},{24,0},{28,4},{1,9},{5... | collective-permute-start | bytes 786440 | tf_op jit(solution)/shard_map/ppermute | solution.py:704
  562.8 45.2 %collective-permute-start.79 = (f32[64,1024]{1,0:T(8,128)S(1)}, f32[64,1024]{1,0:T(8,128)S(1)}, u32[]{:S(2)}, u32[]{:S(2)}) collective-permute-start(f32[64,1024]{1,0:T(8,128)S(1)} %copy-done.56), channel_id=1, source_target_pairs={{0,16},{4,20},{8,24},{12,28},{16,0},{20,4},{24,8},{28,12},{1,17},{... | collective-permute-start | bytes 786440 | tf_op jit(solution)/shard_map/ppermute | solution.py:704
  562.8 55.4 %collective-permute-start.78 = (f32[64,1024]{1,0:T(8,128)S(1)}, f32[64,1024]{1,0:T(8,128)S(1)}, u32[]{:S(2)}, u32[]{:S(2)}) collective-permute-start(f32[64,1024]{1,0:T(8,128)S(1)} %copy-done.56), channel_id=1, source_target_pairs={{0,24},{4,28},{8,0},{12,4},{16,8},{20,12},{24,16},{28,20},{1,25},{... | collective-permute-start | bytes 786440 | tf_op jit(solution)/shard_map/ppermute | solution.py:704
  570.8 47.5 %collective-permute-start.54 = (f32[64,1024]{1,0:T(8,128)S(1)}, f32[64,1024]{1,0:T(8,128)S(1)}, u32[]{:S(2)}, u32[]{:S(2)}) collective-permute-start(f32[64,1024]{1,0:T(8,128)S(1)} %add.409), channel_id=1, source_target_pairs={{0,2},{1,3},{2,0},{3,1},{4,6},{5,7},{6,4},{7,5},{8,10},{9,11},{10,... | collective-permute-start | bytes 786440 | tf_op jit(solution)/shard_map/ppermute | solution.py:643
  573.7 95.0 %collective-permute-start.99 = (f32[4,64,1024]{2,1,0:T(8,128)}, f32[4,64,1024]{2,1,0:T(8,128)}, u32[]{:S(2)}, u32[]{:S(2)}) collective-permute-start(f32[4,64,1024]{2,1,0:T(8,128)} %pad_maximum_fusion.8.refs_1_), channel_id=1, source_target_pairs={{0,4},{4,0},{8,12},{12,8},{16,20},{20,16},{24,28},{28,24},{1,5},{5... | collective-permute-start | bytes 3145736 | tf_op jit(solution)/shard_map/ppermute | solution.py:706
  575.3 93.5 %collective-permute-start.88 = (f32[4,64,1024]{2,1,0:T(8,128)}, f32[4,64,1024]{2,1,0:T(8,128)S(1)}, u32[]{:S(2)}, u32[]{:S(2)}) collective-permute-start(f32[4,64,1024]{2,1,0:T(8,128)} %pad_maximum_fusion.6.refs_1_), channel_id=1, source_target_pairs={{0,1},{1,0},{2,3},{3,2},{4,5},{5,4},{6,7},{7,6},{8,9},{9,8},{10,11... | collective-permute-start | bytes 3145736 | tf_op jit(solution)/shard_map/ppermute | solution.py:640
  608.1 61.7 %collective-permute-start.89 = (f32[4,64,1024]{2,1,0:T(8,128)}, f32[4,64,1024]{2,1,0:T(8,128)S(1)}, u32[]{:S(2)}, u32[]{:S(2)}) collective-permute-start(f32[4,64,1024]{2,1,0:T(8,128)} %collective-permute-done.87.refs_2_), channel_id=1, source_target_pairs={{0,1},{1,0},{2,3},{3,2},{4,5},{5,4},{6,7},{7,6},{8,9},{9,8},{10,11... | collective-permute-start | bytes 3145736 | tf_op jit(solution)/shard_map/ppermute | solution.py:640
  618.3 51.6 %collective-permute-start.94 = (f32[4,64,1024]{2,1,0:T(8,128)}, f32[4,64,1024]{2,1,0:T(8,128)}, u32[]{:S(2)}, u32[]{:S(2)}) collective-permute-start(f32[4,64,1024]{2,1,0:T(8,128)} %pad_maximum_fusion.7.refs_5_), channel_id=1, source_target_pairs={{0,1},{1,0},{2,3},{3,2},{4,5},{5,4},{6,7},{7,6},{8,9},{9,8},{10,11... | collective-permute-start | bytes 3145736 | tf_op jit(solution)/shard_map/ppermute | solution.py:640
  618.3 54.8 %collective-permute-start.95 = (f32[4,64,1024]{2,1,0:T(8,128)}, f32[4,64,1024]{2,1,0:T(8,128)}, u32[]{:S(2)}, u32[]{:S(2)}) collective-permute-start(f32[4,64,1024]{2,1,0:T(8,128)} %collective-permute-done.93.refs_6_), channel_id=1, source_target_pairs={{0,1},{1,0},{2,3},{3,2},{4,5},{5,4},{6,7},{7,6},{8,9},{9,8},{10,11... | collective-permute-start | bytes 3145736 | tf_op jit(solution)/shard_map/ppermute | solution.py:640
  668.7 56.2 %collective-permute-start.105 = (f32[4,64,1024]{2,1,0:T(8,128)}, f32[4,64,1024]{2,1,0:T(8,128)}, u32[]{:S(2)}, u32[]{:S(2)}) collective-permute-start(f32[4,64,1024]{2,1,0:T(8,128)} %pad_maximum_fusion.9.refs_5_), channel_id=1, source_target_pairs={{0,4},{4,0},{8,12},{12,8},{16,20},{20,16},{24,28},{28,24},{1,5},{5... | collective-permute-start | bytes 3145736 | tf_op jit(solution)/shard_map/ppermute | solution.py:706
  668.8 52.4 %collective-permute-start.68 = (f32[64,1024]{1,0:T(8,128)S(1)}, f32[64,1024]{1,0:T(8,128)S(1)}, u32[]{:S(2)}, u32[]{:S(2)}) collective-permute-start(f32[64,1024]{1,0:T(8,128)S(1)} %get-tuple-element.129), channel_id=1, source_target_pairs={{0,8},{4,12},{8,16},{12,20},{16,24},{20,28},{24,0},{28,4},{1,9},{5... | collective-permute-start | bytes 786440 | tf_op jit(solution)/shard_map/ppermute | solution.py:704
  669.8 53.4 %collective-permute-start.67 = (f32[64,1024]{1,0:T(8,128)S(1)}, f32[64,1024]{1,0:T(8,128)S(1)}, u32[]{:S(2)}, u32[]{:S(2)}) collective-permute-start(f32[64,1024]{1,0:T(8,128)S(1)} %get-tuple-element.129), channel_id=1, source_target_pairs={{0,16},{4,20},{8,24},{12,28},{16,0},{20,4},{24,8},{28,12},{1,17},{... | collective-permute-start | bytes 786440 | tf_op jit(solution)/shard_map/ppermute | solution.py:704
  669.8 53.6 %collective-permute-start.66 = (f32[64,1024]{1,0:T(8,128)S(1)}, f32[64,1024]{1,0:T(8,128)S(1)}, u32[]{:S(2)}, u32[]{:S(2)}) collective-permute-start(f32[64,1024]{1,0:T(8,128)S(1)} %get-tuple-element.129), channel_id=1, source_target_pairs={{0,24},{4,28},{8,0},{12,4},{16,8},{20,12},{24,16},{28,20},{1,25},{... | collective-permute-start | bytes 786440 | tf_op jit(solution)/shard_map/ppermute | solution.py:704
  673.1 51.9 %collective-permute-start.55 = (f32[64,1024]{1,0:T(8,128)S(1)}, f32[64,1024]{1,0:T(8,128)S(1)}, u32[]{:S(2)}, u32[]{:S(2)}) collective-permute-start(f32[64,1024]{1,0:T(8,128)S(1)} %add.410), channel_id=1, source_target_pairs={{0,1},{1,0},{2,3},{3,2},{4,5},{5,4},{6,7},{7,6},{8,9},{9,8},{10,11... | collective-permute-start | bytes 786440 | tf_op jit(solution)/shard_map/ppermute | solution.py:640
  721.2 99.6 %collective-permute-start.63 = (f32[4,64,1024]{2,1,0:T(8,128)}, f32[4,64,1024]{2,1,0:T(8,128)}, u32[]{:S(2)}, u32[]{:S(2)}) collective-permute-start(f32[4,64,1024]{2,1,0:T(8,128)} %pad_maximum_fusion.2.refs_1_), channel_id=1, source_target_pairs={{0,4},{4,0},{8,12},{12,8},{16,20},{20,16},{24,28},{28,24},{1,5},{5... | collective-permute-start | bytes 3145736 | tf_op jit(solution)/shard_map/ppermute | solution.py:706
  723.3 30.7 %collective-permute-start.100 = (f32[4,64,1024]{2,1,0:T(8,128)}, f32[4,64,1024]{2,1,0:T(8,128)}, u32[]{:S(2)}, u32[]{:S(2)}) collective-permute-start(f32[4,64,1024]{2,1,0:T(8,128)} %pad_maximum_fusion.8.refs_1_), channel_id=1, source_target_pairs={{0,1},{1,0},{2,3},{3,2},{4,5},{5,4},{6,7},{7,6},{8,9},{9,8},{10,11... | collective-permute-start | bytes 3145736 | tf_op jit(solution)/shard_map/ppermute | solution.py:640
  723.5 32.1 %collective-permute-start.101 = (f32[4,64,1024]{2,1,0:T(8,128)}, f32[4,64,1024]{2,1,0:T(8,128)}, u32[]{:S(2)}, u32[]{:S(2)}) collective-permute-start(f32[4,64,1024]{2,1,0:T(8,128)} %collective-permute-done.99.refs_2_), channel_id=1, source_target_pairs={{0,1},{1,0},{2,3},{3,2},{4,5},{5,4},{6,7},{7,6},{8,9},{9,8},{10,11... | collective-permute-start | bytes 3145736 | tf_op jit(solution)/shard_map/ppermute | solution.py:640
  724.8 32.3 %collective-permute-start.106 = (f32[4,64,1024]{2,1,0:T(8,128)}, f32[4,64,1024]{2,1,0:T(8,128)}, u32[]{:S(2)}, u32[]{:S(2)}) collective-permute-start(f32[4,64,1024]{2,1,0:T(8,128)} %pad_maximum_fusion.9.refs_5_), channel_id=1, source_target_pairs={{0,1},{1,0},{2,3},{3,2},{4,5},{5,4},{6,7},{7,6},{8,9},{9,8},{10,11... | collective-permute-start | bytes 3145736 | tf_op jit(solution)/shard_map/ppermute | solution.py:640
  725.1 32.1 %collective-permute-start.107 = (f32[4,64,1024]{2,1,0:T(8,128)}, f32[4,64,1024]{2,1,0:T(8,128)}, u32[]{:S(2)}, u32[]{:S(2)}) collective-permute-start(f32[4,64,1024]{2,1,0:T(8,128)} %collective-permute-done.105.refs_6_), channel_id=1, source_target_pairs={{0,1},{1,0},{2,3},{3,2},{4,5},{5,4},{6,7},{7,6},{8,9},{9,8},{10,11... | collective-permute-start | bytes 3145736 | tf_op jit(solution)/shard_map/ppermute | solution.py:640
  755.1 53.0 %collective-permute-start.75 = (f32[4,64,1024]{2,1,0:T(8,128)S(1)}, f32[4,64,1024]{2,1,0:T(8,128)}, u32[]{:S(2)}, u32[]{:S(2)}) collective-permute-start(f32[4,64,1024]{2,1,0:T(8,128)S(1)} %copy-done.132), channel_id=1, source_target_pairs={{0,4},{4,0},{8,12},{12,8},{16,20},{20,16},{24,28},{28,24},{1,5},{5... | collective-permute-start | bytes 3145736 | tf_op jit(solution)/shard_map/ppermute | solution.py:706
  755.6 61.3 %collective-permute-start.81 = (f32[4,64,1024]{2,1,0:T(8,128)}, f32[4,64,1024]{2,1,0:T(8,128)}, u32[]{:S(2)}, u32[]{:S(2)}) collective-permute-start(f32[4,64,1024]{2,1,0:T(8,128)} %pad_maximum_fusion.5.refs_5_), channel_id=1, source_target_pairs={{0,4},{4,0},{8,12},{12,8},{16,20},{20,16},{24,28},{28,24},{1,5},{5... | collective-permute-start | bytes 3145736 | tf_op jit(solution)/shard_map/ppermute | solution.py:706
  757.1 49.4 %collective-permute-start.58 = (f32[2,32,1024]{2,1,0:T(8,128)S(1)}, f32[2,32,1024]{2,1,0:T(8,128)S(1)}, u32[]{:S(2)}, u32[]{:S(2)}) collective-permute-start(f32[2,32,1024]{2,1,0:T(8,128)S(1)} %dynamic-slice_bitcast_fusion.10), channel_id=1, source_target_pairs={{0,1},{1,0},{2,3},{3,2},{4,5},{5,4},{6,7},{7,6},{8,9},{9,8},{10,11... | collective-permute-start | bytes 786440 | tf_op jit(solution)/shard_map/ppermute | solution.py:640
  757.1 59.7 %collective-permute-start.56 = (f32[2,256,512]{2,1,0:T(8,128)S(1)}, f32[2,256,512]{2,1,0:T(8,128)}, u32[]{:S(2)}, u32[]{:S(2)}) collective-permute-start(f32[2,256,512]{2,1,0:T(8,128)S(1)} %dynamic-slice_bitcast_fusion), channel_id=1, source_target_pairs={{0,1},{1,0},{2,3},{3,2},{4,5},{5,4},{6,7},{7,6},{8,9},{9,8},{10,11... | collective-permute-start | bytes 3145736 | tf_op jit(solution)/shard_map/ppermute | solution.py:640
  820.8 95.8 %collective-permute-start.64 = (f32[4,64,1024]{2,1,0:T(8,128)}, f32[4,64,1024]{2,1,0:T(8,128)}, u32[]{:S(2)}, u32[]{:S(2)}) collective-permute-start(f32[4,64,1024]{2,1,0:T(8,128)} %pad_maximum_fusion.2.refs_1_), channel_id=1, source_target_pairs={{0,1},{1,0},{2,3},{3,2},{4,5},{5,4},{6,7},{7,6},{8,9},{9,8},{10,11... | collective-permute-start | bytes 3145736 | tf_op jit(solution)/shard_map/ppermute | solution.py:640
  820.9 95.7 %collective-permute-start.65 = (f32[4,64,1024]{2,1,0:T(8,128)}, f32[4,64,1024]{2,1,0:T(8,128)}, u32[]{:S(2)}, u32[]{:S(2)}) collective-permute-start(f32[4,64,1024]{2,1,0:T(8,128)} %collective-permute-done.63.refs_2_), channel_id=1, source_target_pairs={{0,1},{1,0},{2,3},{3,2},{4,5},{5,4},{6,7},{7,6},{8,9},{9,8},{10,11... | collective-permute-start | bytes 3145736 | tf_op jit(solution)/shard_map/ppermute | solution.py:640
  821.4 51.7 %collective-permute-start.35 = (f32[256,512]{1,0:T(8,128)S(1)}, f32[256,512]{1,0:T(8,128)S(1)}, u32[]{:S(2)}, u32[]{:S(2)}) collective-permute-start(f32[256,512]{1,0:T(8,128)S(1)} %copy-done.147), channel_id=1, source_target_pairs={{0,2},{1,3},{2,0},{3,1},{4,6},{5,7},{6,4},{7,5},{8,10},{9,11},{10,... | collective-permute-start | bytes 1572872 | tf_op jit(solution)/shard_map/ppermute | solution.py:643
  822.9 50.2 %collective-permute-start.69 = (f32[4,64,1024]{2,1,0:T(8,128)}, f32[4,64,1024]{2,1,0:T(8,128)}, u32[]{:S(2)}, u32[]{:S(2)}) collective-permute-start(f32[4,64,1024]{2,1,0:T(8,128)} %pad_maximum_fusion.3.refs_5_), channel_id=1, source_target_pairs={{0,4},{4,0},{8,12},{12,8},{16,20},{20,16},{24,28},{28,24},{1,5},{5... | collective-permute-start | bytes 3145736 | tf_op jit(solution)/shard_map/ppermute | solution.py:706
  823.5 50.2 %collective-permute-start.57 = (f32[256,512]{1,0:T(8,128)S(1)}, f32[256,512]{1,0:T(8,128)S(1)}, u32[]{:S(2)}, u32[]{:S(2)}) collective-permute-start(f32[256,512]{1,0:T(8,128)S(1)} %dynamic-slice_bitcast_fusion.5), channel_id=1, source_target_pairs={{0,2},{1,3},{2,0},{3,1},{4,6},{5,7},{6,4},{7,5},{8,10},{9,11},{10,... | collective-permute-start | bytes 1572872 | tf_op jit(solution)/shard_map/ppermute | solution.py:643
  873.1 43.6 %collective-permute-start.70 = (f32[4,64,1024]{2,1,0:T(8,128)}, f32[4,64,1024]{2,1,0:T(8,128)}, u32[]{:S(2)}, u32[]{:S(2)}) collective-permute-start(f32[4,64,1024]{2,1,0:T(8,128)} %pad_maximum_fusion.3.refs_5_), channel_id=1, source_target_pairs={{0,1},{1,0},{2,3},{3,2},{4,5},{5,4},{6,7},{7,6},{8,9},{9,8},{10,11... | collective-permute-start | bytes 3145736 | tf_op jit(solution)/shard_map/ppermute | solution.py:640
  873.2 43.5 %collective-permute-start.71 = (f32[4,64,1024]{2,1,0:T(8,128)}, f32[4,64,1024]{2,1,0:T(8,128)}, u32[]{:S(2)}, u32[]{:S(2)}) collective-permute-start(f32[4,64,1024]{2,1,0:T(8,128)} %collective-permute-done.69.refs_6_), channel_id=1, source_target_pairs={{0,1},{1,0},{2,3},{3,2},{4,5},{5,4},{6,7},{7,6},{8,9},{9,8},{10,11... | collective-permute-start | bytes 3145736 | tf_op jit(solution)/shard_map/ppermute | solution.py:640
  (288 other events, 4586.2 us)
Sparse Core Ops, SparseCore 0:
  524.5 208.6 all-reduce.7
  748.7 142.3 all-reduce.5
